TPU v7x, 256 devices: a whole 4x4x8 slice. The times are simulated.
256 devices in a mesh: dp: 8 (over z_hi, x), expert: 32 (over y, z_lo, core).
Axes of the slice: x: 4, y: 4, z: 8 (z_hi: 2, z_lo: 4; z = z_hi * 4 + z_lo), core: 2. Of those that a mesh axis runs over, the one named last changes fastest.
Arguments:
- tokens: bfloat16 [4096, 3584], P('expert'), may hold values from -6 to 6
- expert_ids: int32 [4096, 8], P('expert'), may hold values from 0 to 31, all different within a row; in each aligned block of 128 rows (0 to 127, 128 to 255, ...) at most 48 rows name the same one
- route_weight: float32 [4096, 8], P('expert'), may hold values from 0.1 to 1
- pair_swap: int32 [16], replicated, may hold values from 0 to 1, as said below
- expert_gate: bfloat16 [32, 3584, 2048], P('expert', None, 'dp'), may hold values from -0.09375 to 0.09375
- expert_up: bfloat16 [32, 3584, 2048], P('expert', None, 'dp'), may hold values from -0.09375 to 0.09375
- expert_down: bfloat16 [32, 2048, 3584], P('expert', 'dp'), may hold values from -0.1875 to 0.1875
- shared_gate: bfloat16 [3584, 2048], P(None, 'dp'), may hold values from -0.09375 to 0.09375
- shared_up: bfloat16 [3584, 2048], P(None, 'dp'), may hold values from -0.09375 to 0.09375
- shared_down: bfloat16 [2048, 3584], P('dp'), may hold values from -0.1875 to 0.1875
Outputs:
- layer_out: bfloat16 [4096, 3584], P('expert', 'dp')
Inputs may be any that keep to these rules, and one draw needn't show every extreme that they name: `expert_ids`: each row names 8 different experts; within the rows of one device (aligned blocks of 128 rows) no expert is named more than 48 times, a bound that some block reaches. `pair_swap`: entry 0 is always 1; the other entries are 0 or 1.
All inputs are finite; a program needn't handle non-finite values.
Results may differ from a plain program's by a relative error of at most 0.012.
Values may be sent and summed in bfloat16 or wider, within the bound.
A program may use at most 192 MiB of HBM per device.

v0:
```python
import jax
import jax.numpy as jnp
from jax import lax
from jax.sharding import PartitionSpec as P

routed_scale = 2.5


def from_partner(value, axis, stride):
    mask = 2**stride
    pairs = [(source, source ^ mask) for source in range(lax.axis_size(axis))]
    return lax.ppermute(value, axis, pairs)


def local(
    tokens,
    expert_ids,
    route_weight,
    pair_swap,
    expert_gate,
    expert_up,
    expert_down,
    shared_gate,
    shared_up,
    shared_down,
):
    tok_count, top_count = expert_ids.shape
    width = tokens.shape[1]
    experts = lax.axis_size("expert")
    half_axis = experts // 2
    capacity = 3 * tok_count * top_count // (2 * experts)
    column = lax.axis_index("expert")
    gate_block = expert_gate[0]
    up_block = expert_up[0]
    down_block = expert_down[0]
    swap_bit = experts.bit_length() - 2
    moved = from_partner((gate_block, up_block, down_block), "expert", swap_bit)
    keep_flag = pair_swap[column % half_axis] == 1
    gate_block = jnp.where(keep_flag, moved[0], gate_block)
    up_block = jnp.where(keep_flag, moved[1], up_block)
    down_block = jnp.where(keep_flag, moved[2], down_block)
    flat_target = expert_ids.reshape(-1)
    onehot = (flat_target[:, None] == jnp.arange(experts, dtype=jnp.int32)[None, :]).astype(
        jnp.int32
    )
    before = jnp.cumsum(onehot, axis=0) - onehot
    slot_index = jnp.sum(before * onehot, axis=1)
    position = flat_target * capacity + slot_index
    owner_row = jnp.arange(tok_count * top_count, dtype=jnp.int32) // top_count
    source_row = jnp.full((experts * capacity,), tok_count, jnp.int32).at[position].set(owner_row)
    padded = jnp.concatenate([tokens, jnp.zeros((1, width), tokens.dtype)], axis=0)
    mix = route_weight / jnp.sum(route_weight, axis=1, keepdims=True)
    shared_gv = jnp.dot(tokens, shared_gate, preferred_element_type=jnp.float32)
    shared_uv = jnp.dot(tokens, shared_up, preferred_element_type=jnp.float32)
    shared_act = (jax.nn.silu(shared_gv) * shared_uv).astype(jnp.bfloat16)
    shared_out = jnp.dot(shared_act, shared_down, preferred_element_type=jnp.float32)
    send_rows = jnp.take(padded, source_row, axis=0).reshape(experts, capacity, width)
    received = lax.all_to_all(send_rows, "expert", split_axis=0, concat_axis=0, tiled=True)
    sources, items, row_width = received.shape
    flat_rows = received.reshape(sources * items, row_width)
    gate_val = jnp.dot(flat_rows, gate_block, preferred_element_type=jnp.float32)
    up_val = jnp.dot(flat_rows, up_block, preferred_element_type=jnp.float32)
    act = (jax.nn.silu(gate_val) * up_val).astype(jnp.bfloat16)
    partial_out = jnp.dot(act, down_block, preferred_element_type=jnp.float32).astype(jnp.bfloat16)
    partial_out = partial_out.reshape(sources, items, row_width)
    returned = lax.all_to_all(partial_out, "expert", split_axis=0, concat_axis=0, tiled=True)
    back_rows = returned.reshape(experts * capacity, width)
    picked = jnp.take(back_rows, position, axis=0).reshape(tok_count, top_count, width)
    routed = jnp.zeros((tok_count, width), jnp.float32)
    for choice_index in range(top_count):
        routed = routed + mix[:, choice_index : choice_index + 1] * picked[:, choice_index].astype(
            jnp.float32
        )
    term = shared_out + routed_scale * routed
    summed = lax.psum_scatter(term, "dp", scatter_dimension=1, tiled=True)
    return summed.astype(jnp.bfloat16)


def solution(mesh):
    in_specs = (
        P("expert", None),
        P("expert", None),
        P("expert", None),
        P(),
        P("expert", None, "dp"),
        P("expert", None, "dp"),
        P("expert", "dp", None),
        P(None, "dp"),
        P(None, "dp"),
        P("dp", None),
    )
    out_specs = P("expert", "dp")
    return jax.shard_map(local, mesh=mesh, in_specs=in_specs, out_specs=out_specs, check_vma=False)
```

profile of v0, /device:TPU:8, one launch (start us, length us, event | category | flops | bytes accessed | tf_op | source)
XLA Modules:
  0.0 712.5 jit_solution(12988139991898341660)
XLA Ops:
  6.5 0.9 copy.18
  7.5 0.1 eq.34
  7.5 0.1 reshape.102
  7.6 0.7 broadcast_multiply_fusion
  8.4 9.0 %reduce-window.6 = s32[32,8,128]{2,1,0:T(8,128)S(1)} reduce-window(s32[32,8,128]{2,1,0:T(8,128)S(1)} %fusion.30, s32[]{:T(128)} %constant.71.clone.1), window={size=1x1x128 pad=0_0x0_0x127_0}, to_apply=%region_1.2 | reduce-window | flops 4161536 | bytes 262148 | tf_op jit(solution)/shard_map/reduce-window
  17.5 0.1 copy.20
  17.7 0.1 broadcast_add_fusion
  17.8 0.1 copy.23
  17.9 0.1 mul.129
  18.1 4.3 scatter_custom_fusion
  22.5 1.2 concatenate.3
  23.8 9.1 %gather_fusion = bf16[1536,3584]{1,0:T(8,128)(2,1)} fusion(bf16[129,3584]{1,0:T(8,128)(2,1)S(1)} %concatenate.3, s32[2048]{0:T(1024)S(1)} %pad_clamp_fusion), kind=kCustom, calls=%fused_computation | custom fusion | bytes 22026240 | tf_op jit(solution)/shard_map/jit(_take)/gather | solution.py:57
  32.9 9.9 %broadcast_select_fusion = bf16[32,48,3584]{2,1,0:T(8,128)(2,1)} fusion(bf16[32,48,3584]{2,1,0:T(8,128)(2,1)} %bitcast.105, pred[32,48]{1,0:T(8,128)(4,1)S(1)} %broadcast_in_dim.33), kind=kLoop, calls=%fused_computation.4 | loop fusion | flops 5505024 | bytes 22021632 | tf_op jit(solution)/shard_map/jit(_take)/select_n | solution.py:57
  42.8 9.3 %all-to-all-start = ((bf16[32,48,3584]{2,1,0:T(8,128)(2,1)}), bf16[32,48,3584]{2,1,0:T(8,128)(2,1)}, u32[]{:S(2)}, u32[]{:S(2)}) async-start(bf16[32,48,3584]{2,1,0:T(8,128)(2,1)} %broadcast_select_fusion), calls=%async_computation | async-start | bytes 22020096 | tf_op jit(solution)/shard_map/all_to_all | solution.py:58
  52.1 2.2 collective-permute-start.1
  54.3 1.4 collective-permute-start
  55.7 2.1 collective-permute-start.2
  57.8 0.6 dynamic_slice.3
  59.0 121.1 %collective-permute-done.1 = bf16[3584,256]{1,0:T(8,128)(2,1)} collective-permute-done((bf16[3584,256]{1,0:T(8,128)(2,1)}, bf16[3584,256]{1,0:T(8,128)(2,1)}, u32[]{:S(2)}, u32[]{:S(2)}) %collective-permute-start.1) | collective-permute-done | bytes 1835040 | tf_op jit(solution)/shard_map/ppermute | solution.py:12
  180.2 111.4 %all-to-all-done = bf16[32,48,3584]{2,1,0:T(8,128)(2,1)} async-done(((bf16[32,48,3584]{2,1,0:T(8,128)(2,1)}), bf16[32,48,3584]{2,1,0:T(8,128)(2,1)}, u32[]{:S(2)}, u32[]{:S(2)}) %all-to-all-start) | async-done | bytes 11010080 | tf_op jit(solution)/shard_map/all_to_all | solution.py:58
  291.6 9.4 %fusion.9 = f32[1536,256]{1,0:T(8,128)} fusion(bf16[1536,3584]{1,0:T(8,128)(2,1)} %bitcast.6, bf16[3584,256]{1,0:T(8,128)(2,1)} %collective-permute-done.1, pred[]{:T(512)} %bitcast.7, bf16[1,3584,256]{2,1,0:T(8,128)(2,1)} %param.15), kind=kOutput, calls=%fused_computation.24 | convolution fusion | flops 2819489792 | bytes 16252929 | tf_op jit(solution)/shard_map/dot_general | solution.py:62
  300.9 19.0 %convolution_convert_fusion = bf16[1536,3584]{1,0:T(8,128)(2,1)} fusion(bf16[256,3584]{1,0:T(8,128)(2,1)} %collective-permute-done.2, pred[]{:T(512)} %bitcast.7, f32[1536,256]{1,0:T(8,128)} %fusion.9, bf16[1536,3584]{1,0:T(8,128)(2,1)} %bitcast.6, bf16[3584,256]{1,0:T(8,128)(2,1)} %collective-permute-done, bf16[1,256,3584]{2,1,0:T(8,128)(2,1)} %param.16, ...), kind=kOutput, calls=%fused_computation.3 | convolution fusion | flops 5646843904 | bytes 30932992 | tf_op jit(solution)/shard_map/dot_general | solution.py:64
  319.9 7.1 all-to-all-start.1
  327.0 0.3 reduce-scatter.2.cloned.1.call-start
  327.5 1.9 fusion.43
  329.4 237.0 %all-to-all-done.1 = bf16[32,48,3584]{2,1,0:T(8,128)(2,1)} async-done(((bf16[32,48,3584]{2,1,0:T(8,128)(2,1)}), bf16[32,48,3584]{2,1,0:T(8,128)(2,1)}, u32[]{:S(2)}, u32[]{:S(2)}) %all-to-all-start.1) | async-done | bytes 11010080 | tf_op jit(solution)/shard_map/all_to_all | solution.py:66
  566.5 19.3 %gather_fusion.1 = bf16[1024,3584]{1,0:T(8,128)(2,1)} fusion(bf16[1536,3584]{1,0:T(8,128)(2,1)} %bitcast.12, s32[1024]{0:T(1024)S(1)} %broadcast_clamp_fusion), kind=kCustom, calls=%fused_computation.1 | custom fusion | bytes 14684160 | tf_op jit(solution)/shard_map/jit(_take)/gather | solution.py:68
  585.8 11.0 %copy.24 = bf16[128,8,3584]{0,2,1:T(8,128)(2,1)} copy(bf16[128,8,3584]{2,1,0:T(8,128)(2,1)} %bitcast.106) | data formatting | bytes 14680064 | tf_op jit(solution)/shard_map/jit(_take)/gather | solution.py:68
  596.8 6.7 broadcast_select_fusion.1
  603.5 7.3 %convolution_add_fusion = f32[128,3584]{0,1:T(8,128)} fusion(bf16[256,3584]{1,0:T(8,128)(2,1)S(1)} %copy-done, bf16[128,3584]{1,0:T(8,128)(2,1)S(1)} %copy-done.1, bf16[3584,256]{1,0:T(8,128)(2,1)} %param.18, bf16[128,8,3584]{0,2,1:T(8,128)(2,1)} %broadcast_select_fusion.1, f32[128]{0:T(128)S(1)} %get-tuple-element.6, f32[128]{0:T(128)S(1)} %get-tuple-element.7, ...), kind=kOutput, calls=%fused_computation.6 | convolution fusion | flops 481427456 | bytes 13897728 | tf_op jit(solution)/shard_map/dot_general | solution.py:56
  610.8 93.3 %reduce-scatter.2.cloned.1.call-done = f32[128,448]{0,1:T(8,128)} async-done(((f32[128,3584]{0,1:T(8,128)}), f32[128,448]{0,1:T(8,128)}) %reduce-scatter.2.cloned.1.call-update) | async-done | bytes 229392 | tf_op jit(solution)/shard_map/reduce_scatter | solution.py:75
  704.1 1.6 convert_element_type.88
  (32 shorter events, 0.6 us)
Async XLA Ops:
  6.5 597.0 %copy-start = (bf16[256,3584]{1,0:T(8,128)(2,1)S(1)}, bf16[256,3584]{1,0:T(8,128)(2,1)}, u32[]{:S(2)}) copy-start(bf16[256,3584]{1,0:T(8,128)(2,1)} %param.19) | copy-start | bytes 5505028
  42.8 15.1 %copy-start.4 = (s32[16]{0:T(128)S(1)}, s32[16]{0:T(128)}, u32[]{:S(2)}) copy-start(s32[16]{0:T(128)} %param.13) | copy-start | bytes 196
  42.8 248.8 %all-to-all-start = ((bf16[32,48,3584]{2,1,0:T(8,128)(2,1)}), bf16[32,48,3584]{2,1,0:T(8,128)(2,1)}, u32[]{:S(2)}, u32[]{:S(2)}) async-start(bf16[32,48,3584]{2,1,0:T(8,128)(2,1)} %broadcast_select_fusion), calls=%async_computation | async-start | bytes 22020096 | tf_op jit(solution)/shard_map/all_to_all | solution.py:58
  52.1 128.1 %collective-permute-start.1 = (bf16[3584,256]{1,0:T(8,128)(2,1)}, bf16[3584,256]{1,0:T(8,128)(2,1)}, u32[]{:S(2)}, u32[]{:S(2)}) collective-permute-start(bf16[3584,256]{1,0:T(8,128)(2,1)} %bitcast.113), channel_id=1, source_target_pairs={{0,16},{1,17},{2,18},{3,19},{4,20},{5,21},{6,22},{7,23},{8,24},{9,... | collective-permute-start | bytes 5505032 | tf_op jit(solution)/shard_map/ppermute | solution.py:12
  54.3 246.7 %collective-permute-start = (bf16[3584,256]{1,0:T(8,128)(2,1)}, bf16[3584,256]{1,0:T(8,128)(2,1)}, u32[]{:S(2)}, u32[]{:S(2)}) collective-permute-start(bf16[3584,256]{1,0:T(8,128)(2,1)} %bitcast.115), channel_id=1, source_target_pairs={{0,16},{1,17},{2,18},{3,19},{4,20},{5,21},{6,22},{7,23},{8,24},{9,... | collective-permute-start | bytes 5505032 | tf_op jit(solution)/shard_map/ppermute | solution.py:12
  55.7 245.2 %collective-permute-start.2 = (bf16[256,3584]{1,0:T(8,128)(2,1)}, bf16[256,3584]{1,0:T(8,128)(2,1)}, u32[]{:S(2)}, u32[]{:S(2)}) collective-permute-start(bf16[256,3584]{1,0:T(8,128)(2,1)} %bitcast.114), channel_id=1, source_target_pairs={{0,16},{1,17},{2,18},{3,19},{4,20},{5,21},{6,22},{7,23},{8,24},{9,... | collective-permute-start | bytes 5505032 | tf_op jit(solution)/shard_map/ppermute | solution.py:12
  319.9 7.5 %copy-start.3 = (f32[128,8]{0,1:T(8,128)S(1)}, f32[128,8]{0,1:T(8,128)}, u32[]{:S(2)}) copy-start(f32[128,8]{0,1:T(8,128)} %param.12) | copy-start | bytes 12292
  319.9 7.6 %copy-start.2 = (s32[128,8]{0,1:T(8,128)S(1)}, s32[128,8]{0,1:T(8,128)}, u32[]{:S(2)}) copy-start(s32[128,8]{0,1:T(8,128)} %param.11) | copy-start | bytes 12292
  319.9 7.6 %copy-start.1 = (bf16[128,3584]{1,0:T(8,128)(2,1)S(1)}, bf16[128,3584]{1,0:T(8,128)(2,1)}, u32[]{:S(2)}) copy-start(bf16[128,3584]{1,0:T(8,128)(2,1)} %param.10) | copy-start | bytes 2752516
  319.9 246.5 %all-to-all-start.1 = ((bf16[32,48,3584]{2,1,0:T(8,128)(2,1)}), bf16[32,48,3584]{2,1,0:T(8,128)(2,1)}, u32[]{:S(2)}, u32[]{:S(2)}) async-start(bf16[32,48,3584]{2,1,0:T(8,128)(2,1)} %bitcast.107), calls=%async_computation.1 | async-start | bytes 22020096 | tf_op jit(solution)/shard_map/all_to_all | solution.py:66
  327.0 377.1 %reduce-scatter.2.cloned.1.call-start = ((), (), s32[]{:S(2)}) async-start(), calls=%async_computation.3 | async-start | bytes 2064384 | tf_op jit(solution)/shard_map/reduce_scatter | solution.py:75
Sparse Core Ops, SparseCore 0:
  610.9 93.1 reduce-scatter.1
where the time goes:
time: 713 us
  waiting for transfers between devices  563 us (79%)
  local copies, waits for them, and re-layouts  47.4 us (7%)
  matrix products  37.5 us (5%)
  other arithmetic  28.2 us (4%)
  starting transfers between devices  22.4 us (3%)
  between operations  14.2 us (2%)
    all_to_all x1, waiting for transfers between devices, local(): lax.all_to_all(partial_out, 'expert', split_axis=0, concat_axis=0, tiled=...  237 us
    ppermute x3, waiting for transfers between devices, from_partner(): return lax.ppermute(value, axis, pairs)  121 us
    all_to_all x1, waiting for transfers between devices, local(): lax.all_to_all(send_rows, 'expert', split_axis=0, concat_axis=0, tiled=True)  111 us
    reduce_scatter x1, waiting for transfers between devices, local(): summed = lax.psum_scatter(term, 'dp', scatter_dimension=1, tiled=True)  93.3 us
    gather x2, local copies, waits for them, and re-layouts, local(): jnp.take(back_rows, position, axis=0).reshape(tok_count, top_count, width)  30.3 us
    dot_general x1, matrix products, local(): jnp.dot(act, down_block, preferred_element_type=jnp.float32)  19 us
  transfers between devices with their start and end apart: 6, of which 4 were waited for; matrix products, arithmetic and copies ran while one was open for 2% of the time, Pallas kernels for 0%

commit v1 on v0

v1 whole, which is shorter than its diff:
```python
import jax
import jax.numpy as jnp
from jax import lax
from jax.sharding import PartitionSpec as P

routed_scale = 2.5


def local(
    tokens,
    expert_ids,
    route_weight,
    pair_swap,
    expert_gate,
    expert_up,
    expert_down,
    shared_gate,
    shared_up,
    shared_down,
):
    f32 = jnp.float32
    rows = tokens.shape[0]
    experts = lax.axis_size("expert")
    half = experts // 2
    columns = jnp.arange(experts, dtype=jnp.int32)
    swap = jnp.concatenate([pair_swap, pair_swap])
    stored = jnp.where(swap == 1, (columns + half) % experts, columns)
    mix = route_weight / jnp.sum(route_weight, axis=1, keepdims=True)
    dense = jnp.sum(
        jnp.where(expert_ids[:, :, None] == stored[None, None, :], routed_scale * mix[:, :, None], 0.0), axis=1
    )
    every = lax.all_gather(tokens, "expert", axis=0, tiled=True)
    mine = lax.all_to_all(dense, "expert", split_axis=1, concat_axis=0, tiled=True)
    gate_val = jnp.dot(every, expert_gate[0], preferred_element_type=f32)
    up_val = jnp.dot(every, expert_up[0], preferred_element_type=f32)
    act = (jax.nn.silu(gate_val) * up_val * mine).astype(jnp.bfloat16)
    part = jnp.dot(act, expert_down[0], preferred_element_type=f32)
    shared_gv = jnp.dot(tokens, shared_gate, preferred_element_type=f32)
    shared_uv = jnp.dot(tokens, shared_up, preferred_element_type=f32)
    shared_act = (jax.nn.silu(shared_gv) * shared_uv).astype(jnp.bfloat16)
    shared_out = jnp.dot(shared_act, shared_down, preferred_element_type=f32)
    first = lax.psum_scatter(part.astype(jnp.bfloat16), "dp", scatter_dimension=1, tiled=True)
    second = lax.psum_scatter(first, "expert", scatter_dimension=0, tiled=True)
    shared_sum = lax.psum_scatter(shared_out.astype(jnp.bfloat16), "dp", scatter_dimension=1, tiled=True)
    return (second.astype(f32) + shared_sum.astype(f32)).astype(jnp.bfloat16)


def solution(mesh):
    in_specs = (
        P("expert", None),
        P("expert", None),
        P("expert", None),
        P(),
        P("expert", None, "dp"),
        P("expert", None, "dp"),
        P("expert", "dp", None),
        P(None, "dp"),
        P(None, "dp"),
        P("dp", None),
    )
    return jax.shard_map(local, mesh=mesh, in_specs=in_specs, out_specs=P("expert", "dp"), check_vma=False)
```

time: 713 us -> 981 us (1.38)
  waiting for transfers between devices: 563 us -> 886 us
  local copies, waits for them, and re-layouts: 47.4 us -> 9.18 us
  other arithmetic: 28.2 us -> 5.16 us
  matrix products: 37.5 us -> 57.5 us
  starting transfers between devices: 22.4 us -> 9.27 us
    reduce_scatter x1 -> x2, waiting for transfers between devices: 93.3 us -> 588 us  [the longest x1 482 us: local(): lax.psum_scatter(part.astype(jnp.bfloat16), 'dp', scatter_dimension=1, ti...]
    all_to_all x2 -> x1, waiting for transfers between devices: 348 us -> 0.01 us  [local(): lax.all_to_all(dense, 'expert', split_axis=1, concat_axis=0, tiled=True)]
    all_gather x0 -> x1, waiting for transfers between devices: none -> 155 us  [local(): every = lax.all_gather(tokens, 'expert', axis=0, tiled=True)]
    unnamed x1 -> x5, waiting for transfers between devices: 0.02 us -> 143 us
    ppermute x3 -> x0, waiting for transfers between devices: 121 us -> none  [from_partner(): return lax.ppermute(value, axis, pairs)]
    gather x3 -> x0, local copies, waits for them, and re-layouts: 39.4 us -> none  [the longest x2 30.3 us: local(): jnp.take(back_rows, position, axis=0).reshape(tok_count, top_count, width)]
    dot_general x4, matrix products: 37.5 us -> 57.5 us  [the longest x1 37.4 us: local(): part = jnp.dot(act, expert_down[0], preferred_element_type=f32)]
    select_n x5 -> x1, other arithmetic: 16.6 us -> 0.81 us  [local(): stored = jnp.where(swap == 1, (columns + half) % experts, columns)]
  transfers between devices with their start and end apart: 6 -> 5, of which waited for: 4 -> 4; matrix products, arithmetic and copies ran while one was open for 2% -> 3% of each run, Pallas kernels for 0% -> 0%
where the time goes in v1:
time: 981 us
  waiting for transfers between devices  886 us (90%)
  matrix products  57.5 us (6%)
  between operations  13.2 us (1%)
    reduce_scatter x1, waiting for transfers between devices, local(): lax.psum_scatter(part.astype(jnp.bfloat16), 'dp', scatter_dimension=1, ti...  482 us
    all_gather x1, waiting for transfers between devices, local(): every = lax.all_gather(tokens, 'expert', axis=0, tiled=True)  155 us
    unnamed x5, waiting for transfers between devices  143 us
    reduce_scatter x1, waiting for transfers between devices, local(): lax.psum_scatter(shared_out.astype(jnp.bfloat16), 'dp', scatter_dimension...  106 us
    dot_general x1, matrix products, local(): part = jnp.dot(act, expert_down[0], preferred_element_type=f32)  37.4 us
  transfers between devices with their start and end apart: 5, of which 4 were waited for; matrix products, arithmetic and copies ran while one was open for 3% of the time, Pallas kernels for 0%

profile of v1, /device:TPU:8, one launch (start us, length us, event | category | flops | bytes accessed | tf_op | source)
XLA Modules:
  0.0 980.6 jit_solution(4599210068851855276)
XLA Ops:
  6.5 0.0 copy-start
  6.5 0.0 all-gather.2.cloned.1.call-start
  6.5 0.7 all-gather.2.cloned.1.call-update
  7.3 0.7 reduce_sum.18
  8.0 0.8 compare_select_fusion.2
  8.8 0.7 divide_multiply_fusion
  9.5 1.4 select_reduce_fusion
  10.8 9.1 all-to-all-start
  20.0 0.0 reduce-scatter.6.cloned.1.call-start
  20.0 155.0 %all-gather.2.cloned.1.call-done = bf16[4096,3584]{1,0:T(8,128)(2,1)} async-done(((bf16[128,3584]{1,0:T(8,128)(2,1)}), bf16[4096,3584]{1,0:T(8,128)(2,1)}) %all-gather.2.cloned.1.call-update) | async-done | bytes 29360144 | tf_op jit(solution)/shard_map/all_gather | solution.py:32
  175.0 15.2 %fusion.7 = f32[4096,256]{1,0:T(8,128)} fusion(bf16[4096,3584]{1,0:T(8,128)(2,1)} %all-gather.2.cloned.1.call-done, bf16[1,3584,256]{2,1,0:T(8,128)(2,1)} %param.14), kind=kOutput, calls=%fused_computation.9 | convolution fusion | flops 7516192768 | bytes 35389440 | tf_op jit(solution)/shard_map/dot_general | solution.py:34
  190.2 0.0 all-to-all-done
  190.2 0.0 copy-done
  190.2 37.4 %convolution_convert_fusion = bf16[4096,3584]{0,1:T(8,128)(2,1)} fusion(bf16[4096,3584]{1,0:T(8,128)(2,1)} %all-gather.2.cloned.1.call-done, f32[4096,256]{1,0:T(8,128)} %fusion.7, f32[4096]{0:T(1024)S(1)} %bitcast.26, bf16[1,256,3584]{2,1,0:T(8,128)(2,1)S(1)} %copy-done, bf16[1,3584,256]{2,1,0:T(8,128)(2,1)} %param.15), kind=kOutput, calls=%fused_computation | convolution fusion | flops 15054405632 | bytes 66600960 | tf_op jit(solution)/shard_map/dot_general | solution.py:37
  227.6 0.0 reduce-scatter.6.cloned.1.call-update
  227.6 0.0 reduce-scatter.10.cloned.1.call-start
  227.6 482.4 %reduce-scatter.6.cloned.1.call-done = bf16[4096,448]{0,1:T(8,128)(2,1)} async-done(((bf16[4096,3584]{0,1:T(8,128)(2,1)}), bf16[4096,448]{0,1:T(8,128)(2,1)}) %reduce-scatter.6.cloned.1.call-update) | async-done | bytes 3670032 | tf_op jit(solution)/shard_map/reduce_scatter | solution.py:42
  710.0 6.4 copy.20
  716.4 0.0 copy-start.2
  716.4 0.0 reduce-scatter.10.cloned.1.call-update
  716.4 0.0 reduce-scatter.8.cloned.1.call-start
  716.5 1.1 copy-done.2
  717.6 0.6 copy-done.3
  718.2 0.4 fusion.19
  718.6 0.0 copy-start.1
  718.6 4.6 convolution_convert_fusion.1
  723.2 0.0 reduce-scatter.8.cloned.1.call-update
  723.2 142.2 %reduce-scatter.10.cloned.1.call-done = bf16[128,448]{1,0:T(8,128)(2,1)} async-done(((bf16[4096,448]{1,0:T(8,128)(2,1)}), bf16[128,448]{1,0:T(8,128)(2,1)}) %reduce-scatter.10.cloned.1.call-update) | async-done | bytes 114704
  865.5 1.0 copy.21
  866.5 106.0 %reduce-scatter.8.cloned.1.call-done = bf16[128,448]{0,1:T(8,128)(2,1)} async-done(((bf16[128,3584]{0,1:T(8,128)(2,1)}), bf16[128,448]{0,1:T(8,128)(2,1)}) %reduce-scatter.8.cloned.1.call-update) | async-done | bytes 114704 | tf_op jit(solution)/shard_map/reduce_scatter | solution.py:44
  972.5 1.6 add_convert_fusion
  974.1 0.0 copy-done.1
  (1 shorter events, 0.0 us)
Async XLA Ops:
  6.5 183.7 %copy-start = (bf16[1,256,3584]{2,1,0:T(8,128)(2,1)S(1)}, bf16[1,256,3584]{2,1,0:T(8,128)(2,1)}, u32[]{:S(2)}) copy-start(bf16[1,256,3584]{2,1,0:T(8,128)(2,1)} %param.16) | copy-start | bytes 5505028
  6.5 168.5 %all-gather.2.cloned.1.call-start = ((), (), s32[]{:S(2)}) async-start(), calls=%async_computation.4 | async-start | bytes 30277632 | tf_op jit(solution)/shard_map/all_gather | solution.py:32
  10.8 179.3 %all-to-all-start = ((f32[128,32,1]{0,2,1:T(1,128)}), f32[128,32,1]{0,2,1:T(1,128)S(1)}, u32[]{:S(2)}, u32[]{:S(2)}) async-start(f32[128,32,1]{0,2,1:T(1,128)} %bitcast.3), calls=%async_computation | async-start | bytes 32768 | tf_op jit(solution)/shard_map/all_to_all | solution.py:33
  20.0 690.0 %reduce-scatter.6.cloned.1.call-start = ((), (), s32[]{:S(2)}) async-start(), calls=%async_computation.5 | async-start | bytes 33030144 | tf_op jit(solution)/shard_map/reduce_scatter | solution.py:42
  227.6 637.9 %reduce-scatter.10.cloned.1.call-start = ((), (), s32[]{:S(2)}) async-start(), calls=%async_computation.7 | async-start | bytes 4325376
  716.4 1.2 copy-start.2
  716.4 1.8 copy-start.3
  716.4 256.1 %reduce-scatter.8.cloned.1.call-start = ((), (), s32[]{:S(2)}) async-start(), calls=%async_computation.6 | async-start | bytes 1032192 | tf_op jit(solution)/shard_map/reduce_scatter | solution.py:44
  718.6 255.5 %copy-start.1 = (bf16[1,256,3584]{2,1,0:T(8,128)(2,1)S(1)}, bf16[1,256,3584]{2,1,0:T(8,128)(2,1)}, u32[]{:S(2)}) copy-start(bf16[1,256,3584]{2,1,0:T(8,128)(2,1)} %param.16) | copy-start | bytes 5505028
Sparse Core Ops, SparseCore 0:
  9.2 165.7 all-gather.1
  227.7 482.2 reduce-scatter.5
  716.6 148.8 reduce-scatter.9
  869.8 102.6 reduce-scatter.7

commit v2 on v1

v2 whole, which is shorter than its diff:
```python
import functools

import jax
import jax.numpy as jnp
from jax import lax
from jax.experimental import pallas as pl
from jax.experimental.pallas import tpu as pltpu
from jax.sharding import PartitionSpec as P

MESH = pl.DeviceIdType.MESH
F32 = jnp.float32
BF16 = jnp.bfloat16
routed_scale = 2.5
D = 3584
TOK = 128
HID = 256
C1 = (0, 896)
C2 = (896, 1152)
QBASE, QW = 2048, 384
ROWS = (48, 48, 32)
OFFS = (0, 48, 96)
XC = 896
SPLIT = (32, 32, 16)


class Place:
    def __init__(self):
        self.dp = lax.axis_index("dp")
        self.ex = lax.axis_index("expert")
        self.x = self.dp % 4
        self.zh = self.dp // 4
        self.y = self.ex // 8
        self.k = (self.ex // 2) % 4
        self.c = self.ex % 2
        self.z = self.zh * 4 + self.k

    def xn(self, d):
        return (self.zh * 4 + (self.x + d + 4) % 4, self.ex)

    def yn(self, d):
        return (self.dp, ((self.y + d + 4) % 4) * 8 + self.k * 2 + self.c)

    def zn(self, d):
        z = (self.z + d + 8) % 8
        return ((z // 4) * 4 + self.x, self.y * 8 + (z % 4) * 2 + self.c)

    def peer(self):
        return (self.dp, self.ex + 1 - 2 * self.c)

    def plane(self, q):
        return (self.dp, q * 2 + self.c)


class Links:
    def __init__(self, send_sem, recv_sem):
        self.send_sem, self.recv_sem, self.count = send_sem, recv_sem, 0
        self.sent = []

    def slot(self):
        self.count += 1
        return self.count - 1

    def start(self, slot, src, dst, dev):
        copy = pltpu.make_async_remote_copy(
            src_ref=src, dst_ref=dst, send_sem=self.send_sem.at[slot], recv_sem=self.recv_sem.at[slot],
            device_id=dev, device_id_type=MESH)
        copy.start()
        self.sent.append(copy)

    def wait(self, slot, dst, dev):
        pltpu.make_async_remote_copy(
            src_ref=dst, dst_ref=dst, send_sem=self.send_sem.at[slot], recv_sem=self.recv_sem.at[slot],
            device_id=dev, device_id_type=MESH).wait_recv()

    def drain(self):
        for copy in self.sent:
            copy.wait_send()
        self.sent = []


class Gather:
    def __init__(self, links, unit, nb, i, own=None):
        self.links, self.unit, self.nb, self.i = links, unit, nb, i
        self.own = own or (lambda h: unit(i, h))
        self.s = [links.slot() for _ in range(6)]

    def send(self):
        l, u, i, s, nb = self.links, self.unit, self.i, self.s, self.nb
        l.start(s[0], self.own(0), u(i, 0), nb(1))
        l.start(s[1], self.own(1), u(i, 1), nb(-1))
        l.start(s[2], self.own(1), u(i, 1), nb(1))
        l.start(s[3], self.own(0), u(i, 0), nb(-1))

    def forward(self):
        l, u, s, nb = self.links, self.unit, self.s, self.nb
        left, right = (self.i + 3) % 4, (self.i + 1) % 4
        l.wait(s[0], u(left, 0), nb(-1))
        l.start(s[4], u(left, 0), u(left, 0), nb(1))
        l.wait(s[1], u(right, 1), nb(1))
        l.start(s[5], u(right, 1), u(right, 1), nb(-1))

    def near(self):
        l, u, s, nb = self.links, self.unit, self.s, self.nb
        left, right = (self.i + 3) % 4, (self.i + 1) % 4
        l.wait(s[2], u(left, 1), nb(-1))
        l.wait(s[3], u(right, 0), nb(1))

    def far(self):
        l, u, s, nb = self.links, self.unit, self.s, self.nb
        opp = (self.i + 2) % 4
        l.wait(s[4], u(opp, 0), nb(-1))
        l.wait(s[5], u(opp, 1), nb(1))


def greet(devices):
    barrier = pltpu.get_barrier_semaphore()
    for dev in devices:
        pl.semaphore_signal(barrier, inc=1, device_id=dev, device_id_type=MESH)
    pl.semaphore_wait(barrier, len(devices))


def k1_body(tokens, wt, gate, up, down, sgate, sup,
            act_a, act_b, act_c, sact, down_peer,
            X, T, W, SW, WT, acc, send_sem, recv_sem, local_sem, wt_send, wt_recv):
    me = Place()
    x, y, k = me.x, me.y, me.k
    q_me = y * 4 + k
    qx = pl.ds(pl.multiple_of(QBASE + QW * x, 128), QW)
    c1 = pl.ds(C1[0], C1[1])
    c2 = pl.ds(C2[0], C2[1])
    both = pl.ds(0, QBASE)

    locals_ = [
        pltpu.make_async_copy(tokens.at[:, both], X.at[y, k, :, both], local_sem.at[0]),
        pltpu.make_async_copy(tokens.at[:, qx], X.at[y, k, :, qx], local_sem.at[1]),
        pltpu.make_async_copy(gate, W.at[0], local_sem.at[2]),
        pltpu.make_async_copy(up, W.at[2], local_sem.at[3]),
        pltpu.make_async_copy(tokens, T, local_sem.at[4]),
        pltpu.make_async_copy(sgate, SW.at[0], local_sem.at[5]),
        pltpu.make_async_copy(sup, SW.at[1], local_sem.at[6]),
    ]
    for copy in locals_:
        copy.start()

    hops = [me.plane((q_me + d) % 16) for d in range(1, 16)]
    greet(hops + [me.xn(1), me.xn(-1), me.zn(1), me.zn(-1), me.peer()])

    links = Links(send_sem, recv_sem)

    def rows(h):
        return pl.ds(64 * h, 64)

    def two(h):
        return pl.ds(2 * h, 2)

    g3y = Gather(links, lambda u, h: X.at[u, k, rows(h), qx], me.yn, y, lambda h: tokens.at[rows(h), qx])
    g1y = Gather(links, lambda u, h: X.at[u, k, rows(h), c1], me.yn, y, lambda h: tokens.at[rows(h), c1])
    g2z = Gather(links, lambda u, h: X.at[y, u, rows(h), c2], me.zn, k, lambda h: tokens.at[rows(h), c2])
    g3z = Gather(links, lambda u, h: X.at[two(h), u, :, qx], me.zn, k)
    g1z = Gather(links, lambda u, h: X.at[two(h), u, :, c1], me.zn, k)
    g2y = Gather(links, lambda u, h: X.at[u, two(h), :, c2], me.yn, y)

    def qcol(u):
        return pl.ds(pl.multiple_of(QBASE + QW * u, 128), QW)

    g3x = [Gather(links, functools.partial(lambda s, u, h: X.at[two(h), s, :, qcol(u)], (k + d) % 4), me.xn, x)
           for d in range(4)]

    g3y.send()
    g1y.send()
    g2z.send()
    for d in range(1, 16):
        q = (q_me + d) % 16
        pltpu.make_async_remote_copy(
            src_ref=wt.at[q], dst_ref=WT.at[q_me], send_sem=wt_send.at[d], recv_sem=wt_recv.at[d],
            device_id=me.plane(q), device_id_type=MESH).start()
    WT[q_me] = wt[q_me]
    peer = me.peer()
    swaps = []
    for n, (src, dst) in enumerate(((gate, W.at[1]), (up, W.at[3]), (down, down_peer))):
        slot = links.slot()
        swaps.append((slot, dst))
        links.start(slot, src, dst, peer)

    locals_[0].wait()
    locals_[1].wait()
    g3y.forward()
    g3y.near()
    g3y.far()
    g3z.send()
    g3x[0].send()
    g2z.forward()
    g1y.forward()
    acc[...] = jnp.zeros_like(acc)
    g2z.near()
    g2z.far()
    g2y.send()
    g1y.near()
    g1y.far()
    g1z.send()

    def dots(part, read, cols, write):
        lo, width = cols

        def step(n, carry):
            res = jnp.dot(read(lo, width), W[n, lo:lo + width, :], preferred_element_type=F32)
            write(n, res)
            return carry

        lax.fori_loop(0, 4, step, 0)

    def by_column(s, cols):
        def read(lo, width):
            return X[:, s, :, lo:lo + width].reshape(4 * TOK, width)

        def write(n, res):
            acc[n, :, s] += res.reshape(4, TOK, HID)

        dots(0, read, cols, write)

    def by_row(u, cols):
        def read(lo, width):
            return X[u, :, :, lo:lo + width].reshape(4 * TOK, width)

        def write(n, res):
            acc[n, u] += res.reshape(4, TOK, HID)

        dots(0, read, cols, write)

    g3x[0].forward()
    for copy in locals_[2:]:
        copy.wait()
    sg = jnp.dot(T[...], SW[0], preferred_element_type=F32)
    su = jnp.dot(T[...], SW[1], preferred_element_type=F32)
    sact[...] = (sg / (1.0 + jnp.exp(-sg)) * su).astype(BF16)
    g3z.forward()
    g3x[0].near()
    g3z.near()
    g3x[1].send()
    g3x[3].send()
    g3x[0].far()
    g3z.far()
    g3x[2].send()
    for slot, dst in swaps[:2]:
        links.wait(slot, dst, peer)
    by_column(k, C1)
    g3x[1].forward()
    g3x[3].forward()
    by_column(k, (QBASE, D - QBASE))
    by_row(y, C2)
    g1z.forward()
    g2y.forward()
    g3x[2].forward()
    g3x[1].near()
    g3x[1].far()
    by_column((k + 1) % 4, (QBASE, D - QBASE))
    g3x[3].near()
    g3x[3].far()
    by_column((k + 3) % 4, (QBASE, D - QBASE))
    g1z.near()
    by_column((k + 1) % 4, C1)
    by_column((k + 3) % 4, C1)
    g2y.near()
    by_row((y + 1) % 4, C2)
    by_row((y + 3) % 4, C2)
    g3x[2].near()
    g3x[2].far()
    by_column((k + 2) % 4, (QBASE, D - QBASE))
    g1z.far()
    by_column((k + 2) % 4, C1)
    g2y.far()
    by_row((y + 2) % 4, C2)

    for d in range(1, 16):
        q = (q_me + 16 - d) % 16
        pltpu.make_async_remote_copy(
            src_ref=wt.at[q], dst_ref=WT.at[q], send_sem=wt_send.at[d], recv_sem=wt_recv.at[d],
            device_id=me.plane(q), device_id_type=MESH).wait()

    def finish(b, carry):
        yb, kb = b // 4, b % 4
        w = jnp.transpose(WT[b])
        halves = []
        for n in range(2):
            g = acc[n, yb, kb]
            u = acc[2 + n, yb, kb]
            halves.append((g / (1.0 + jnp.exp(-g)) * u * w[:, n:n + 1]).astype(BF16))
        for n in range(2):
            hs = pl.ds(n * HID, HID)
            act_a[yb, kb, :, hs] = halves[n][0:48]
            act_b[yb, kb, :, hs] = halves[n][48:96]
            act_c[kb, yb, :, hs] = halves[n][96:128]
        return carry

    lax.fori_loop(0, 16, finish, 0)
    links.wait(swaps[2][0], swaps[2][1], peer)
    links.drain()


class Reduce:
    def __init__(self, links, part, bufs, nb, i, add, add3):
        self.links, self.part, self.bufs, self.nb, self.i = links, part, bufs, nb, i
        self.add, self.add3 = add, add3
        self.s = [links.slot() for _ in range(6)]

    def t(self, d):
        return (self.i + d + 4) % 4

    def first(self):
        l, p, b, s = self.links, self.part, self.bufs, self.s
        l.start(s[0], p(self.t(2), 0), b(0), self.nb(1))
        l.start(s[1], p(self.t(2), 1), b(1), self.nb(-1))

    def second_right(self):
        self.links.start(self.s[2], self.part(self.t(1), 1), self.bufs(2), self.nb(1))

    def second_left(self):
        self.links.start(self.s[3], self.part(self.t(-1), 0), self.bufs(3), self.nb(-1))

    def third(self):
        l, p, b, s = self.links, self.part, self.bufs, self.s
        l.wait(s[0], b(0), self.nb(-1))
        self.add(p(self.t(1), 0), b(0))
        l.start(s[4], p(self.t(1), 0), b(4), self.nb(1))
        l.wait(s[1], b(1), self.nb(1))
        self.add(p(self.t(-1), 1), b(1))
        l.start(s[5], p(self.t(-1), 1), b(5), self.nb(-1))

    def last(self):
        l, p, b, s = self.links, self.part, self.bufs, self.s
        l.wait(s[3], b(3), self.nb(1))
        l.wait(s[4], b(4), self.nb(-1))
        self.add3(p(self.i, 0), b(3), b(4))
        l.wait(s[2], b(2), self.nb(-1))
        l.wait(s[5], b(5), self.nb(1))
        self.add3(p(self.i, 1), b(2), b(5))


def k2_body(act_a, act_b, act_c, sact, down, down_peer, sdown, out,
            PA, PB, PC, A1, A2, A3, A4, B1, B2, B3, B4, CC1, CC2, CC3, CC4,
            DW, SD, F, E, G, send_sem, recv_sem):
    me = Place()
    x, y, k = me.x, me.y, me.k
    greet([me.xn(1), me.xn(-1), me.yn(1), me.yn(-1), me.zn(1), me.zn(-1), me.zn(4)])
    links = Links(send_sem, recv_sem)

    def add2d(dst, a):
        dst[...] = (dst[...].astype(F32) + a[...].astype(F32)).astype(BF16)

    def add3_2d(dst, a, b):
        dst[...] = (dst[...].astype(F32) + a[...].astype(F32) + b[...].astype(F32)).astype(BF16)

    def add3d(dst, a):
        lax.fori_loop(0, dst.shape[0], lambda n, t: (add2d(dst.at[n], a.at[n]), t)[1], 0)

    def add3_3d(dst, a, b):
        lax.fori_loop(0, dst.shape[0], lambda n, t: (add3_2d(dst.at[n], a.at[n], b.at[n]), t)[1], 0)

    def add4d(dst, a):
        w = dst.shape[1]
        lax.fori_loop(0, dst.shape[0] * w, lambda n, t: (add2d(dst.at[n // w, n % w], a.at[n // w, n % w]), t)[1], 0)

    def add3_4d(dst, a, b):
        w = dst.shape[1]
        lax.fori_loop(
            0, dst.shape[0] * w,
            lambda n, t: (add3_2d(dst.at[n // w, n % w], a.at[n // w, n % w], b.at[n // w, n % w]), t)[1], 0)

    def permute(dst, src, base):
        for xx in range(4):
            dst[xx, base:base + HID] = jnp.concatenate(
                [src[:, 448 * xx:448 * xx + 448], src[:, 1792 + 448 * xx:1792 + 448 * xx + 448]], axis=1)

    permute(DW, down, 0)
    permute(DW, down_peer, HID)
    permute(SD, sdown, 0)

    NS = ((0, 256), (256, 256), (512, 256), (768, 128))

    def shared(xx, off, rows):
        return jnp.dot(sact[off:off + rows, :], SD[xx], preferred_element_type=F32)

    def down_a(t):
        def body(m, carry):
            lhs = act_a[pl.ds(2 * m, 2)].reshape(8 * 48, 512)
            for lo, w in NS:
                r = jnp.dot(lhs, DW[t, :, lo:lo + w], preferred_element_type=F32)
                PA[t, pl.ds(2 * m, 2), :, :, lo:lo + w] = r.astype(BF16).reshape(2, 4, 48, w)
            return carry
        lax.fori_loop(0, 2, body, 0)
        PA[t, y, k] = (PA[t, y, k].astype(F32) + shared(t, 0, 48)).astype(BF16)

    def down_b(t):
        def body(xx, carry):
            lhs = act_b[t].reshape(4 * 48, 512)
            for lo, w in NS:
                r = jnp.dot(lhs, DW[xx, :, lo:lo + w], preferred_element_type=F32)
                PB[t, :, xx, :, lo:lo + w] = r.astype(BF16).reshape(4, 48, w)
            return carry
        lax.fori_loop(0, 4, body, 0)

    def down_c(t):
        def body(xx, carry):
            lhs = act_c[t].reshape(4 * 32, 512)
            for lo, w in NS:
                r = jnp.dot(lhs, DW[xx, :, lo:lo + w], preferred_element_type=F32)
                PC[t, xx, :, :, lo:lo + w] = r.astype(BF16).reshape(4, 32, w)
            return carry
        lax.fori_loop(0, 4, body, 0)

    def two(h):
        return pl.ds(2 * h, 2)

    def part_rows(p, h):
        return pl.ds(0, SPLIT[p]) if h == 0 else pl.ds(SPLIT[p], ROWS[p] - SPLIT[p])

    def last_bufs(p, pair):
        return lambda n: pair[0].at[n // 2] if n in (0, 3, 4) else pair[1].at[n // 2]

    ra = Reduce(links, lambda t, h: PA.at[t, two(h)], lambda n: A1.at[n], me.xn, x, add4d, add3_4d)
    rb = Reduce(links, lambda t, h: PB.at[t, two(h)], lambda n: B1.at[n], me.yn, y, add4d, add3_4d)
    rc = Reduce(links, lambda t, h: PC.at[t, two(h)], lambda n: CC1.at[n], me.zn, k, add4d, add3_4d)
    down_a((x + 2) % 4)
    ra.first()
    down_b((y + 2) % 4)
    rb.first()
    down_c((k + 2) % 4)
    rc.first()
    down_a((x + 1) % 4)
    ra.second_right()
    down_a((x + 3) % 4)
    ra.second_left()
    down_b((y + 1) % 4)
    rb.second_right()
    down_b((y + 3) % 4)
    rb.second_left()
    down_c((k + 1) % 4)
    rc.second_right()
    down_c((k + 3) % 4)
    rc.second_left()
    ra.third()
    rb.third()
    rc.third()
    down_a(x)
    down_b(y)
    down_c(k)

    def own_shared(xx, carry):
        PB[y, k, xx] = (PB[y, k, xx].astype(F32) + shared(xx, 48, 48)).astype(BF16)
        PC[k, xx, y] = (PC[k, xx, y].astype(F32) + shared(xx, 96, 32)).astype(BF16)
        return carry

    lax.fori_loop(0, 4, own_shared, 0)

    def run(stages):
        for st in stages:
            st.first()
        for st in stages:
            st.second_right()
            st.second_left()
        for st in stages:
            st.third()

    ra.last()
    rb.last()
    rc.last()
    sa = Reduce(links, lambda t, h: PA.at[x, t, two(h)], lambda n: A2.at[n], me.yn, y, add3d, add3_3d)
    sb = Reduce(links, lambda t, h: PB.at[y, t, two(h)], lambda n: B2.at[n], me.zn, k, add3d, add3_3d)
    sc = Reduce(links, lambda t, h: PC.at[k, t, two(h)], lambda n: CC2.at[n], me.xn, x, add3d, add3_3d)
    run((sa, sb, sc))
    sa.last()
    sb.last()
    sc.last()
    ta = Reduce(links, lambda t, h: PA.at[x, y, t, part_rows(0, h)], last_bufs(0, (A3, A4)), me.zn, k, add2d, add3_2d)
    tb = Reduce(links, lambda t, h: PB.at[y, k, t, part_rows(1, h)], last_bufs(1, (B3, B4)), me.xn, x, add2d, add3_2d)
    tc = Reduce(links, lambda t, h: PC.at[k, x, t, part_rows(2, h)], last_bufs(2, (CC3, CC4)), me.yn, y, add2d, add3_2d)
    run((ta, tb, tc))
    ta.last()
    tb.last()
    tc.last()
    F[0:48] = PA[x, y, k]
    F[48:96] = PB[y, k, x]
    F[96:128] = PC[k, x, y]
    lo = F[:, 0:448].astype(F32)
    hi = F[:, 448:896].astype(F32)
    low = me.zh == 0
    E[...] = jnp.where(low, hi, lo).astype(BF16)
    slot = links.slot()
    links.start(slot, E, G, me.zn(4))
    links.wait(slot, G, me.zn(4))
    out[...] = (jnp.where(low, lo, hi) + G[...].astype(F32)).astype(BF16)
    links.drain()


VM = pl.BlockSpec(memory_space=pltpu.VMEM)
ANY = pl.BlockSpec(memory_space=pl.ANY)


def local(tokens, expert_ids, route_weight, pair_swap, expert_gate, expert_up, expert_down,
          shared_gate, shared_up, shared_down):
    core = lax.axis_index("expert") % 2
    swap = pair_swap.reshape(8, 2)
    swap = jnp.where(core == 1, swap[:, ::-1], swap)
    swap = jnp.concatenate([swap, swap], axis=0)
    column = jnp.arange(32, dtype=jnp.int32).reshape(16, 2)
    column = jnp.where(core == 1, column[:, ::-1], column)
    stored = jnp.where(swap == 1, (column + 16) % 32, column)
    stored = jnp.pad(stored, ((0, 0), (0, 6)), constant_values=-1)
    mix = routed_scale * (route_weight / jnp.sum(route_weight, axis=1, keepdims=True))
    wt = jnp.sum(
        jnp.where(expert_ids.T[:, None, None, :] == stored[None, :, :, None], mix.T[:, None, None, :], 0.0), axis=0)

    shape = jax.ShapeDtypeStruct
    scratch = pltpu.VMEM
    dma = pltpu.SemaphoreType.DMA
    act_a, act_b, act_c, sact, down_peer = pl.pallas_call(
        k1_body,
        name="gather_gate_up",
        out_shape=(shape((4, 4, 48, 512), BF16), shape((4, 4, 48, 512), BF16), shape((4, 4, 32, 512), BF16),
                   shape((TOK, HID), BF16), shape((HID, D), BF16)),
        in_specs=[ANY, VM, ANY, ANY, ANY, ANY, ANY],
        out_specs=(VM, VM, VM, VM, ANY),
        scratch_shapes=[
            scratch((4, 4, TOK, D), BF16),
            scratch((TOK, D), BF16),
            scratch((4, D, HID), BF16),
            scratch((2, D, HID), BF16),
            scratch((16, 8, TOK), F32),
            scratch((4, 4, 4, TOK, HID), F32),
            dma((64,)), dma((64,)), dma((8,)), dma((16,)), dma((16,)),
        ],
        compiler_params=pltpu.CompilerParams(collective_id=0, has_side_effects=True, vmem_limit_bytes=58 << 20),
    )(tokens, wt, expert_gate[0], expert_up[0], expert_down[0], shared_gate, shared_up)

    return pl.pallas_call(
        k2_body,
        name="down_reduce",
        out_shape=shape((TOK, 448), BF16),
        in_specs=[VM] * 7,
        out_specs=VM,
        scratch_shapes=[
            scratch((4, 4, 4, 48, XC), BF16), scratch((4, 4, 4, 48, XC), BF16), scratch((4, 4, 4, 32, XC), BF16),
            scratch((6, 2, 4, 48, XC), BF16), scratch((6, 2, 48, XC), BF16),
            scratch((3, 32, XC), BF16), scratch((3, 16, XC), BF16),
            scratch((6, 2, 4, 48, XC), BF16), scratch((6, 2, 48, XC), BF16),
            scratch((3, 32, XC), BF16), scratch((3, 16, XC), BF16),
            scratch((6, 2, 4, 32, XC), BF16), scratch((6, 2, 32, XC), BF16),
            scratch((3, 16, XC), BF16), scratch((3, 16, XC), BF16),
            scratch((4, 512, XC), BF16), scratch((4, HID, XC), BF16),
            scratch((TOK, XC), BF16), scratch((TOK, 448), BF16), scratch((TOK, 448), BF16),
            dma((64,)), dma((64,)),
        ],
        compiler_params=pltpu.CompilerParams(collective_id=1, has_side_effects=True, vmem_limit_bytes=58 << 20),
    )(act_a, act_b, act_c, sact, expert_down[0], down_peer, shared_down)


def solution(mesh):
    in_specs = (
        P("expert", None),
        P("expert", None),
        P("expert", None),
        P(),
        P("expert", None, "dp"),
        P("expert", None, "dp"),
        P("expert", "dp", None),
        P(None, "dp"),
        P(None, "dp"),
        P("dp", None),
    )
    return jax.shard_map(local, mesh=mesh, in_specs=in_specs, out_specs=P("expert", "dp"), check_vma=False)
```

time: 981 us -> 191 us (0.19)
  waiting for transfers between devices: 886 us -> 0 us
  Pallas kernels: 0 us -> 184 us
  matrix products: 57.5 us -> 0 us
  between operations: 13.2 us -> 0.02 us
    reduce_scatter x2 -> x0, waiting for transfers between devices: 588 us -> none  [the longest x1 482 us: local(): lax.psum_scatter(part.astype(jnp.bfloat16), 'dp', scatter_dimension=1, ti...]
    pallas_call x0 -> x2, Pallas kernels: none -> 184 us  [the longest x1 99.2 us: local(): pl.pallas_call(k1_body, name='gather_gate_up', out_shape=(shape((4, 4, 48...]
    all_gather x1 -> x0, waiting for transfers between devices: 155 us -> none  [local(): every = lax.all_gather(tokens, 'expert', axis=0, tiled=True)]
    unnamed x5 -> x0, waiting for transfers between devices: 143 us -> none
    dot_general x4 -> x0, matrix products: 57.5 us -> none  [the longest x1 37.4 us: local(): part = jnp.dot(act, expert_down[0], preferred_element_type=f32)]
  transfers between devices with their start and end apart: 5 -> 0, of which waited for: 4 -> 0; matrix products, arithmetic and copies ran while one was open for 3% -> 0% of each run, Pallas kernels for 0% -> 0%
where the time goes in v2:
time: 191 us; the launch traced here: 190 us
  Pallas kernels  184 us (96%)
  other arithmetic  2.93 us (2%)
  local copies, waits for them, and re-layouts  2.69 us (1%)
    pallas_call x1, Pallas kernels, local(): pl.pallas_call(k1_body, name='gather_gate_up', out_shape=(shape((4, 4, 48...  99.2 us
    pallas_call x1, Pallas kernels, local(): pl.pallas_call(k2_body, name='down_reduce', out_shape=shape((TOK, 448), B...  85 us

profile of v2, /device:TPU:8, one launch (start us, length us, event | category | flops | bytes accessed | tf_op | source)
XLA Modules:
  0.0 189.8 jit_solution(9046297280420886177)
XLA Ops:
  0.0 0.7 reduce_sum.18
  0.7 0.7 multiply_bitcast_fusion
  1.4 0.7 reshape.18
  2.2 0.1 rev.6
  2.2 0.1 copy.17
  2.3 0.1 compare_select_fusion.2
  2.4 0.1 copy.21
  2.5 1.4 select_reduce_fusion.wt
  4.0 99.2 %gather_gate_up.1 = (bf16[4,4,48,512]{3,2,1,0:T(8,128)(2,1)}, bf16[4,4,48,512]{3,2,1,0:T(8,128)(2,1)}, bf16[4,4,32,512]{3,2,1,0:T(8,128)(2,1)}, bf16[128,256]{1,0:T(8,128)(2,1)}, bf16[256,3584]{1,0:T(8,128)(2,1)}) custom-call(bf16[128,3584]{1,0:T(8,128)(2,1)} %tokens.1, f32[16,8,128]{2,1,0:T(8,128)} %select_reduce_fusion.wt, bf16[3584,256]{1,0:T(8,128)(2,1)} %bitcast.8, ...), custom_call_target="tpu_custom_call" | custom-call | tf_op jit(solution)/shard_map/gather_gate_up/pallas_call | solution.py:516
  103.2 85.0 %down_reduce.1 = bf16[128,448]{1,0:T(8,128)(2,1)} custom-call(bf16[4,4,48,512]{3,2,1,0:T(8,128)(2,1)} %get-tuple-element.10.act_a, bf16[4,4,48,512]{3,2,1,0:T(8,128)(2,1)} %get-tuple-element.11.act_b, bf16[4,4,32,512]{3,2,1,0:T(8,128)(2,1)} %get-tuple-element.12.act_c, bf16[128,256]{1,0:T(8,128)(2,1)} %get-tuple-element.13.sact, bf16[256,3584]{1,0:T(8,128)(2,1)} %bitcast.7, ...), custom_call_target="tpu_custom_call" | custom-call | tf_op jit(solution)/shard_map/down_reduce/pallas_call | solution.py:535
  188.2 1.7 copy.20
  (4 shorter events, 0.0 us)

commit v3 on v2

--- a/solution.py
+++ b/solution.py
@@ -119,33 +119,36 @@
     pl.semaphore_wait(barrier, len(devices))
 
 
-def k1_body(tokens, wt, gate, up, down, sgate, sup,
-            act_a, act_b, act_c, sact, down_peer,
-            X, T, W, SW, WT, acc, send_sem, recv_sem, local_sem, wt_send, wt_recv):
-    me = Place()
+def gather_phase(me, links, tokens, ids, rw, swap, gate, up, down, sgate, sup, sdown, act, DW, S, sem,
+                 X, W, SW, RAW, acc, WT, wt, T):
     x, y, k = me.x, me.y, me.k
     q_me = y * 4 + k
-    qx = pl.ds(pl.multiple_of(QBASE + QW * x, 128), QW)
     c1 = pl.ds(C1[0], C1[1])
     c2 = pl.ds(C2[0], C2[1])
     both = pl.ds(0, QBASE)
-
-    locals_ = [
-        pltpu.make_async_copy(tokens.at[:, both], X.at[y, k, :, both], local_sem.at[0]),
-        pltpu.make_async_copy(tokens.at[:, qx], X.at[y, k, :, qx], local_sem.at[1]),
-        pltpu.make_async_copy(gate, W.at[0], local_sem.at[2]),
-        pltpu.make_async_copy(up, W.at[2], local_sem.at[3]),
-        pltpu.make_async_copy(tokens, T, local_sem.at[4]),
-        pltpu.make_async_copy(sgate, SW.at[0], local_sem.at[5]),
-        pltpu.make_async_copy(sup, SW.at[1], local_sem.at[6]),
-    ]
-    for copy in locals_:
+    act_a, act_b, act_c = act
+    local_sem, wt_send, wt_recv = sem
+
+    def qcol(u):
+        return pl.ds(pl.multiple_of(QBASE + QW * u, 128), QW)
+
+    qx = qcol(x)
+
+    def load(src, dst, n):
+        copy = pltpu.make_async_copy(src, dst, local_sem.at[n])
         copy.start()
+        return copy
+
+    own0 = load(tokens.at[:, both], X.at[y, k, :, both], 0)
+    own1 = load(tokens.at[:, qx], X.at[y, k, :, qx], 1)
+    w_gate = load(gate, W.at[0], 2)
+    w_up = load(up, W.at[2], 3)
+    w_down = load(down, RAW, 4)
+    w_sg = load(sgate, SW, 5)
+    w_tok = load(tokens, T, 6)
 
     hops = [me.plane((q_me + d) % 16) for d in range(1, 16)]
-    greet(hops + [me.xn(1), me.xn(-1), me.zn(1), me.zn(-1), me.peer()])
-
-    links = Links(send_sem, recv_sem)
+    greet(hops + [me.xn(1), me.xn(-1), me.yn(1), me.yn(-1), me.zn(1), me.zn(-1), me.zn(4), me.peer()])
 
     def rows(h):
         return pl.ds(64 * h, 64)
@@ -153,147 +156,195 @@
     def two(h):
         return pl.ds(2 * h, 2)
 
+    def row(d):
+        return (y + d) % 4
+
+    def col(d):
+        return (k + d) % 4
+
+    part = functools.partial
     g3y = Gather(links, lambda u, h: X.at[u, k, rows(h), qx], me.yn, y, lambda h: tokens.at[rows(h), qx])
     g1y = Gather(links, lambda u, h: X.at[u, k, rows(h), c1], me.yn, y, lambda h: tokens.at[rows(h), c1])
     g2z = Gather(links, lambda u, h: X.at[y, u, rows(h), c2], me.zn, k, lambda h: tokens.at[rows(h), c2])
-    g3z = Gather(links, lambda u, h: X.at[two(h), u, :, qx], me.zn, k)
-    g1z = Gather(links, lambda u, h: X.at[two(h), u, :, c1], me.zn, k)
-    g2y = Gather(links, lambda u, h: X.at[u, two(h), :, c2], me.yn, y)
-
-    def qcol(u):
-        return pl.ds(pl.multiple_of(QBASE + QW * u, 128), QW)
-
-    g3x = [Gather(links, functools.partial(lambda s, u, h: X.at[two(h), s, :, qcol(u)], (k + d) % 4), me.xn, x)
-           for d in range(4)]
-
+    g3z = [Gather(links, part(lambda s, u, h: X.at[s, u, rows(h), qx], row(d)), me.zn, k,
+                  (lambda h: tokens.at[rows(h), qx]) if d == 0 else None) for d in range(4)]
+    g1z = [Gather(links, part(lambda s, u, h: X.at[s, u, rows(h), c1], row(d)), me.zn, k,
+                  (lambda h: tokens.at[rows(h), c1]) if d == 0 else None) for d in range(4)]
+    g2y = [Gather(links, part(lambda s, u, h: X.at[u, s, rows(h), c2], col(d)), me.yn, y,
+                  (lambda h: tokens.at[rows(h), c2]) if d == 0 else None) for d in range(4)]
+    g3x = [Gather(links, part(lambda s, u, h: X.at[s, two(h), :, qcol(u)], row(d)), me.xn, x) for d in range(4)]
+
+    def done(g):
+        g.near()
+        g.far()
+
+    def dots(read, write, cols):
+        lo, width = cols
+
+        def step(n, carry):
+            write(n, jnp.dot(read(lo, width), W[n, lo:lo + width, :], preferred_element_type=F32))
+            return carry
+
+        lax.fori_loop(0, 4, step, 0)
+
+    def by_column(s, cols):
+        def write(n, res):
+            acc[n, :, s] += res.reshape(4, TOK, HID)
+
+        dots(lambda lo, width: X[:, s, :, lo:lo + width].reshape(4 * TOK, width), write, cols)
+
+    def by_row(u, cols):
+        def write(n, res):
+            acc[n, u] += res.reshape(4, TOK, HID)
+
+        dots(lambda lo, width: X[u, :, :, lo:lo + width].reshape(4 * TOK, width), write, cols)
+
+    QC = (QBASE, D - QBASE)
+
+    g3z[0].send()
     g3y.send()
+    peer = me.peer()
+    swap_gate, swap_up, swap_down = links.slot(), links.slot(), links.slot()
+    links.start(swap_gate, gate, W.at[1], peer)
+    links.start(swap_up, up, W.at[3], peer)
+    weight = rw[...]
+    mix = routed_scale * (weight / jnp.sum(weight, axis=0, keepdims=True))
+    chosen = ids[...]
+    lane_row = lax.broadcasted_iota(jnp.int32, (8, TOK), 0)
+    for q in range(16):
+        tile = jnp.zeros((8, TOK), F32)
+        for r, column in enumerate((2 * q + me.c, 2 * q + 1 - me.c)):
+            stored = (column + 16 * swap[column % 16]) % 32
+            picked = jnp.sum(jnp.where(chosen == stored, mix, 0.0), axis=0, keepdims=True)
+            tile = jnp.where(lane_row == r, picked, tile)
+        wt[q] = tile
+    own0.wait()
+    own1.wait()
+    g3z[0].forward()
+    g3y.forward()
     g1y.send()
-    g2z.send()
+    g3y.near()
+    g3z[1].send()
+    g3z[3].send()
+    done(g3z[0])
+    g3x[0].send()
+    g3y.far()
+    g3z[2].send()
+    g2y[0].send()
     for d in range(1, 16):
         q = (q_me + d) % 16
         pltpu.make_async_remote_copy(
             src_ref=wt.at[q], dst_ref=WT.at[q_me], send_sem=wt_send.at[d], recv_sem=wt_recv.at[d],
             device_id=me.plane(q), device_id_type=MESH).start()
     WT[q_me] = wt[q_me]
-    peer = me.peer()
-    swaps = []
-    for n, (src, dst) in enumerate(((gate, W.at[1]), (up, W.at[3]), (down, down_peer))):
-        slot = links.slot()
-        swaps.append((slot, dst))
-        links.start(slot, src, dst, peer)
-
-    locals_[0].wait()
-    locals_[1].wait()
-    g3y.forward()
-    g3y.near()
-    g3y.far()
-    g3z.send()
-    g3x[0].send()
+    g3z[1].forward()
+    g3z[3].forward()
+    g2z.send()
+    g3z[2].forward()
+    g1z[0].send()
+    w_down.wait()
+    for xx in range(4):
+        DW[xx, 0:HID] = jnp.concatenate(
+            [RAW[:, 448 * xx:448 * xx + 448], RAW[:, 1792 + 448 * xx:1792 + 448 * xx + 448]], axis=1)
+    links.start(swap_down, DW.at[:, pl.ds(0, HID)], DW.at[:, pl.ds(HID, HID)], peer)
+    w_sdown = load(sdown, RAW, 4)
+    g1y.forward()
+    g3x[0].forward()
+    done(g3z[1])
+    g3x[1].send()
+    done(g3z[3])
+    g3x[3].send()
+    done(g3z[2])
+    g3x[2].send()
     g2z.forward()
-    g1y.forward()
     acc[...] = jnp.zeros_like(acc)
+    g1y.near()
+    g1z[1].send()
+    g1z[3].send()
+    g1y.far()
+    g1z[2].send()
+    w_tok.wait()
+    w_sg.wait()
+    sg = jnp.dot(T[...], SW[...], preferred_element_type=F32)
+    w_su = load(sup, SW, 5)
+    silu = sg / (1.0 + jnp.exp(-sg))
     g2z.near()
+    g2y[1].send()
+    g2y[3].send()
+    g2y[0].forward()
+    g1z[0].forward()
     g2z.far()
-    g2y.send()
-    g1y.near()
-    g1y.far()
-    g1z.send()
-
-    def dots(part, read, cols, write):
-        lo, width = cols
-
-        def step(n, carry):
-            res = jnp.dot(read(lo, width), W[n, lo:lo + width, :], preferred_element_type=F32)
-            write(n, res)
-            return carry
-
-        lax.fori_loop(0, 4, step, 0)
-
-    def by_column(s, cols):
-        def read(lo, width):
-            return X[:, s, :, lo:lo + width].reshape(4 * TOK, width)
-
-        def write(n, res):
-            acc[n, :, s] += res.reshape(4, TOK, HID)
-
-        dots(0, read, cols, write)
-
-    def by_row(u, cols):
-        def read(lo, width):
-            return X[u, :, :, lo:lo + width].reshape(4 * TOK, width)
-
-        def write(n, res):
-            acc[n, u] += res.reshape(4, TOK, HID)
-
-        dots(0, read, cols, write)
-
-    g3x[0].forward()
-    for copy in locals_[2:]:
-        copy.wait()
-    sg = jnp.dot(T[...], SW[0], preferred_element_type=F32)
-    su = jnp.dot(T[...], SW[1], preferred_element_type=F32)
-    sact[...] = (sg / (1.0 + jnp.exp(-sg)) * su).astype(BF16)
-    g3z.forward()
-    g3x[0].near()
-    g3z.near()
-    g3x[1].send()
-    g3x[3].send()
-    g3x[0].far()
-    g3z.far()
-    g3x[2].send()
-    for slot, dst in swaps[:2]:
-        links.wait(slot, dst, peer)
-    by_column(k, C1)
+    g2y[2].send()
+    w_su.wait()
+    sact = (silu * jnp.dot(T[...], SW[...], preferred_element_type=F32)).astype(BF16)
+    w_gate.wait()
+    w_up.wait()
+    links.wait(swap_gate, W.at[1], peer)
+    links.wait(swap_up, W.at[3], peer)
+    done(g3x[0])
+    by_row(y, QC)
     g3x[1].forward()
+    done(g1z[0])
+    by_row(y, C1)
+    done(g2y[0])
+    g2y[1].forward()
+    g1z[1].forward()
+    by_column(k, C2)
+    w_sdown.wait()
+    for xx in range(4):
+        S[xx] = jnp.concatenate(
+            [jnp.dot(sact, RAW[:, base + 448 * xx:base + 448 * xx + 448], preferred_element_type=F32)
+             for base in (0, 1792)], axis=1).astype(BF16)
+    g2y[3].forward()
+    g1z[3].forward()
     g3x[3].forward()
-    by_column(k, (QBASE, D - QBASE))
-    by_row(y, C2)
-    g1z.forward()
-    g2y.forward()
+    done(g2y[1])
+    by_column(col(1), C2)
+    done(g3x[1])
+    by_row(row(1), QC)
+    done(g1z[1])
+    by_row(row(1), C1)
+    g2y[2].forward()
+    g1z[2].forward()
     g3x[2].forward()
-    g3x[1].near()
-    g3x[1].far()
-    by_column((k + 1) % 4, (QBASE, D - QBASE))
-    g3x[3].near()
-    g3x[3].far()
-    by_column((k + 3) % 4, (QBASE, D - QBASE))
-    g1z.near()
-    by_column((k + 1) % 4, C1)
-    by_column((k + 3) % 4, C1)
-    g2y.near()
-    by_row((y + 1) % 4, C2)
-    by_row((y + 3) % 4, C2)
-    g3x[2].near()
-    g3x[2].far()
-    by_column((k + 2) % 4, (QBASE, D - QBASE))
-    g1z.far()
-    by_column((k + 2) % 4, C1)
-    g2y.far()
-    by_row((y + 2) % 4, C2)
-
+    done(g2y[3])
+    by_column(col(3), C2)
+    done(g3x[3])
+    by_row(row(3), QC)
+    done(g1z[3])
+    by_row(row(3), C1)
     for d in range(1, 16):
         q = (q_me + 16 - d) % 16
         pltpu.make_async_remote_copy(
             src_ref=wt.at[q], dst_ref=WT.at[q], send_sem=wt_send.at[d], recv_sem=wt_recv.at[d],
             device_id=me.plane(q), device_id_type=MESH).wait()
 
-    def finish(b, carry):
-        yb, kb = b // 4, b % 4
-        w = jnp.transpose(WT[b])
-        halves = []
-        for n in range(2):
-            g = acc[n, yb, kb]
-            u = acc[2 + n, yb, kb]
-            halves.append((g / (1.0 + jnp.exp(-g)) * u * w[:, n:n + 1]).astype(BF16))
-        for n in range(2):
-            hs = pl.ds(n * HID, HID)
-            act_a[yb, kb, :, hs] = halves[n][0:48]
-            act_b[yb, kb, :, hs] = halves[n][48:96]
-            act_c[kb, yb, :, hs] = halves[n][96:128]
-        return carry
-
-    lax.fori_loop(0, 16, finish, 0)
-    links.wait(swaps[2][0], swaps[2][1], peer)
+    def finish(yb):
+        def body(kb, carry):
+            w = jnp.transpose(WT[yb * 4 + kb])
+            for n in range(2):
+                g = acc[n, yb, kb]
+                u = acc[2 + n, yb, kb]
+                v = (g / (1.0 + jnp.exp(-g)) * u * w[:, n:n + 1]).astype(BF16)
+                hs = pl.ds(n * HID, HID)
+                act_a[yb, kb, :, hs] = v[0:48]
+                act_b[yb, kb, :, hs] = v[48:96]
+                act_c[kb, yb, :, hs] = v[96:128]
+            return carry
+
+        lax.fori_loop(0, 4, body, 0)
+
+    done(g2y[2])
+    by_column(col(2), C2)
+    finish(y)
+    finish(row(1))
+    finish(row(3))
+    done(g1z[2])
+    by_row(row(2), C1)
+    done(g3x[2])
+    by_row(row(2), QC)
+    finish(row(2))
+    links.wait(swap_down, DW.at[:, pl.ds(HID, HID)], peer)
     links.drain()
 
 
@@ -336,13 +387,10 @@
         self.add3(p(self.i, 1), b(2), b(5))
 
 
-def k2_body(act_a, act_b, act_c, sact, down, down_peer, sdown, out,
-            PA, PB, PC, A1, A2, A3, A4, B1, B2, B3, B4, CC1, CC2, CC3, CC4,
-            DW, SD, F, E, G, send_sem, recv_sem):
-    me = Place()
+def reduce_phase(me, links, act, DW, S, bufs, F, E, G, out, PA, PB, PC):
     x, y, k = me.x, me.y, me.k
-    greet([me.xn(1), me.xn(-1), me.yn(1), me.yn(-1), me.zn(1), me.zn(-1), me.zn(4)])
-    links = Links(send_sem, recv_sem)
+    act_a, act_b, act_c = act
+    (A1, A2, A3, A4), (B1, B2, B3, B4), (CC1, CC2, CC3, CC4) = bufs
 
     def add2d(dst, a):
         dst[...] = (dst[...].astype(F32) + a[...].astype(F32)).astype(BF16)
@@ -366,19 +414,10 @@
             0, dst.shape[0] * w,
             lambda n, t: (add3_2d(dst.at[n // w, n % w], a.at[n // w, n % w], b.at[n // w, n % w]), t)[1], 0)
 
-    def permute(dst, src, base):
-        for xx in range(4):
-            dst[xx, base:base + HID] = jnp.concatenate(
-                [src[:, 448 * xx:448 * xx + 448], src[:, 1792 + 448 * xx:1792 + 448 * xx + 448]], axis=1)
-
-    permute(DW, down, 0)
-    permute(DW, down_peer, HID)
-    permute(SD, sdown, 0)
-
     NS = ((0, 256), (256, 256), (512, 256), (768, 128))
 
     def shared(xx, off, rows):
-        return jnp.dot(sact[off:off + rows, :], SD[xx], preferred_element_type=F32)
+        return S[xx, off:off + rows, :].astype(F32)
 
     def down_a(t):
         def body(m, carry):
@@ -492,66 +531,53 @@
     links.drain()
 
 
+def layer_body(tokens, ids, rw, swap, gate, up, down, sgate, sup, sdown, out,
+               act_a, act_b, act_c, DW, S, A1, A2, A3, A4, B1, B2, B3, B4, CC1, CC2, CC3, CC4, F, E, G,
+               send_sem, recv_sem, local_sem, wt_send, wt_recv):
+    me = Place()
+    links = Links(send_sem, recv_sem)
+    act = (act_a, act_b, act_c)
+    vmem = pltpu.VMEM
+    pl.run_scoped(
+        functools.partial(gather_phase, me, links, tokens, ids, rw, swap, gate, up, down, sgate, sup, sdown, act, DW, S,
+                          (local_sem, wt_send, wt_recv)),
+        vmem((4, 4, TOK, D), BF16), vmem((4, D, HID), BF16), vmem((D, HID), BF16), vmem((HID, D), BF16),
+        vmem((4, 4, 4, TOK, HID), F32), vmem((16, 8, TOK), F32), vmem((16, 8, TOK), F32), vmem((TOK, D), BF16))
+    pl.run_scoped(
+        functools.partial(reduce_phase, me, links, act, DW, S,
+                          ((A1, A2, A3, A4), (B1, B2, B3, B4), (CC1, CC2, CC3, CC4)), F, E, G, out),
+        vmem((4, 4, 4, 48, XC), BF16), vmem((4, 4, 4, 48, XC), BF16), vmem((4, 4, 4, 32, XC), BF16))
+
+
 VM = pl.BlockSpec(memory_space=pltpu.VMEM)
 ANY = pl.BlockSpec(memory_space=pl.ANY)
 
 
 def local(tokens, expert_ids, route_weight, pair_swap, expert_gate, expert_up, expert_down,
           shared_gate, shared_up, shared_down):
-    core = lax.axis_index("expert") % 2
-    swap = pair_swap.reshape(8, 2)
-    swap = jnp.where(core == 1, swap[:, ::-1], swap)
-    swap = jnp.concatenate([swap, swap], axis=0)
-    column = jnp.arange(32, dtype=jnp.int32).reshape(16, 2)
-    column = jnp.where(core == 1, column[:, ::-1], column)
-    stored = jnp.where(swap == 1, (column + 16) % 32, column)
-    stored = jnp.pad(stored, ((0, 0), (0, 6)), constant_values=-1)
-    mix = routed_scale * (route_weight / jnp.sum(route_weight, axis=1, keepdims=True))
-    wt = jnp.sum(
-        jnp.where(expert_ids.T[:, None, None, :] == stored[None, :, :, None], mix.T[:, None, None, :], 0.0), axis=0)
-
     shape = jax.ShapeDtypeStruct
     scratch = pltpu.VMEM
     dma = pltpu.SemaphoreType.DMA
-    act_a, act_b, act_c, sact, down_peer = pl.pallas_call(
-        k1_body,
-        name="gather_gate_up",
-        out_shape=(shape((4, 4, 48, 512), BF16), shape((4, 4, 48, 512), BF16), shape((4, 4, 32, 512), BF16),
-                   shape((TOK, HID), BF16), shape((HID, D), BF16)),
-        in_specs=[ANY, VM, ANY, ANY, ANY, ANY, ANY],
-        out_specs=(VM, VM, VM, VM, ANY),
-        scratch_shapes=[
-            scratch((4, 4, TOK, D), BF16),
-            scratch((TOK, D), BF16),
-            scratch((4, D, HID), BF16),
-            scratch((2, D, HID), BF16),
-            scratch((16, 8, TOK), F32),
-            scratch((4, 4, 4, TOK, HID), F32),
-            dma((64,)), dma((64,)), dma((8,)), dma((16,)), dma((16,)),
-        ],
-        compiler_params=pltpu.CompilerParams(collective_id=0, has_side_effects=True, vmem_limit_bytes=58 << 20),
-    )(tokens, wt, expert_gate[0], expert_up[0], expert_down[0], shared_gate, shared_up)
-
     return pl.pallas_call(
-        k2_body,
-        name="down_reduce",
+        layer_body,
+        name="expert_layer",
         out_shape=shape((TOK, 448), BF16),
-        in_specs=[VM] * 7,
+        in_specs=[ANY, VM, VM, pl.BlockSpec(memory_space=pltpu.SMEM), ANY, ANY, ANY, ANY, ANY, ANY],
         out_specs=VM,
         scratch_shapes=[
-            scratch((4, 4, 4, 48, XC), BF16), scratch((4, 4, 4, 48, XC), BF16), scratch((4, 4, 4, 32, XC), BF16),
+            scratch((4, 4, 48, 512), BF16), scratch((4, 4, 48, 512), BF16), scratch((4, 4, 32, 512), BF16),
+            scratch((4, 512, XC), BF16), scratch((4, TOK, XC), BF16),
             scratch((6, 2, 4, 48, XC), BF16), scratch((6, 2, 48, XC), BF16),
             scratch((3, 32, XC), BF16), scratch((3, 16, XC), BF16),
             scratch((6, 2, 4, 48, XC), BF16), scratch((6, 2, 48, XC), BF16),
             scratch((3, 32, XC), BF16), scratch((3, 16, XC), BF16),
             scratch((6, 2, 4, 32, XC), BF16), scratch((6, 2, 32, XC), BF16),
             scratch((3, 16, XC), BF16), scratch((3, 16, XC), BF16),
-            scratch((4, 512, XC), BF16), scratch((4, HID, XC), BF16),
             scratch((TOK, XC), BF16), scratch((TOK, 448), BF16), scratch((TOK, 448), BF16),
-            dma((64,)), dma((64,)),
+            dma((192,)), dma((192,)), dma((8,)), dma((16,)), dma((16,)),
         ],
-        compiler_params=pltpu.CompilerParams(collective_id=1, has_side_effects=True, vmem_limit_bytes=58 << 20),
-    )(act_a, act_b, act_c, sact, expert_down[0], down_peer, shared_down)
+        compiler_params=pltpu.CompilerParams(collective_id=0, has_side_effects=True, vmem_limit_bytes=63 << 20),
+    )(tokens, expert_ids.T, route_weight.T, pair_swap, expert_gate[0], expert_up[0], expert_down[0], shared_gate, shared_up, shared_down)
 
 
 def solution(mesh):

time: 191 us -> 169 us (0.88)
  Pallas kernels: 184 us -> 167 us
  other arithmetic: 2.93 us -> 0 us
    pallas_call x2 -> x1, Pallas kernels: 184 us -> 167 us  [local(): pl.pallas_call(layer_body, name='expert_layer', out_shape=shape((TOK, 448...]
    reduce_sum x2 -> x0, other arithmetic: 2.15 us -> none  [the longest x1 1.45 us: local(): jnp.sum(jnp.where(expert_ids.T[:, None, None, :] == stored[None, :, :, No...]
where the time goes in v3:
time: 169 us
  Pallas kernels  167 us (99%)
    pallas_call x1, Pallas kernels, local(): pl.pallas_call(layer_body, name='expert_layer', out_shape=shape((TOK, 448...  167 us

profile of v3, /device:TPU:8, one launch (start us, length us, event | category | flops | bytes accessed | tf_op | source)
XLA Modules:
  0.0 169.0 jit_solution(10178884046970385715)
XLA Ops:
  0.0 167.3 %expert_layer.1 = bf16[128,448]{1,0:T(8,128)(2,1)} custom-call(bf16[128,3584]{1,0:T(8,128)(2,1)} %tokens.1, s32[8,128]{1,0:T(8,128)} %bitcast.8, f32[8,128]{1,0:T(8,128)} %bitcast.9, s32[16]{0:T(128)} %swap.1, bf16[3584,256]{1,0:T(8,128)(2,1)} %bitcast.5, bf16[3584,256]{1,0:T(8,128)(2,1)} %bitcast.6, bf16[256,3584]{1,0:T(8,128)(2,1)} %bitcast.7, ...), custom_call_target="tpu_custom_call" | custom-call | tf_op jit(solution)/shard_map/expert_layer/pallas_call | solution.py:561
  167.3 1.7 copy.11

commit v4 on v3

--- a/solution.py
+++ b/solution.py
@@ -252,17 +252,13 @@
     g3x[0].forward()
     done(g3z[1])
     g3x[1].send()
-    done(g3z[3])
-    g3x[3].send()
-    done(g3z[2])
-    g3x[2].send()
     g2z.forward()
     acc[...] = jnp.zeros_like(acc)
     g1y.near()
     g1z[1].send()
-    g1z[3].send()
     g1y.far()
-    g1z[2].send()
+    done(g3z[3])
+    done(g3z[2])
     w_tok.wait()
     w_sg.wait()
     sg = jnp.dot(T[...], SW[...], preferred_element_type=F32)
@@ -270,11 +266,12 @@
     silu = sg / (1.0 + jnp.exp(-sg))
     g2z.near()
     g2y[1].send()
-    g2y[3].send()
     g2y[0].forward()
+    g3x[1].forward()
+    g3x[3].send()
     g1z[0].forward()
+    g1z[3].send()
     g2z.far()
-    g2y[2].send()
     w_su.wait()
     sact = (silu * jnp.dot(T[...], SW[...], preferred_element_type=F32)).astype(BF16)
     w_gate.wait()
@@ -283,32 +280,35 @@
     links.wait(swap_up, W.at[3], peer)
     done(g3x[0])
     by_row(y, QC)
-    g3x[1].forward()
-    done(g1z[0])
-    by_row(y, C1)
+    g2y[1].forward()
+    g2y[3].send()
     done(g2y[0])
-    g2y[1].forward()
+    by_column(k, C2)
     g1z[1].forward()
-    by_column(k, C2)
+    g1z[2].send()
+    g3x[3].forward()
+    g3x[2].send()
     w_sdown.wait()
     for xx in range(4):
         S[xx] = jnp.concatenate(
             [jnp.dot(sact, RAW[:, base + 448 * xx:base + 448 * xx + 448], preferred_element_type=F32)
              for base in (0, 1792)], axis=1).astype(BF16)
-    g2y[3].forward()
-    g1z[3].forward()
-    g3x[3].forward()
+    done(g1z[0])
+    by_row(y, C1)
     done(g2y[1])
     by_column(col(1), C2)
+    g2y[3].forward()
+    g2y[2].send()
     done(g3x[1])
     by_row(row(1), QC)
+    g1z[3].forward()
     done(g1z[1])
     by_row(row(1), C1)
     g2y[2].forward()
-    g1z[2].forward()
     g3x[2].forward()
     done(g2y[3])
     by_column(col(3), C2)
+    g1z[2].forward()
     done(g3x[3])
     by_row(row(3), QC)
     done(g1z[3])
@@ -459,27 +459,27 @@
     ra = Reduce(links, lambda t, h: PA.at[t, two(h)], lambda n: A1.at[n], me.xn, x, add4d, add3_4d)
     rb = Reduce(links, lambda t, h: PB.at[t, two(h)], lambda n: B1.at[n], me.yn, y, add4d, add3_4d)
     rc = Reduce(links, lambda t, h: PC.at[t, two(h)], lambda n: CC1.at[n], me.zn, k, add4d, add3_4d)
+    down_b((y + 2) % 4)
+    rb.first()
     down_a((x + 2) % 4)
     ra.first()
-    down_b((y + 2) % 4)
-    rb.first()
     down_c((k + 2) % 4)
     rc.first()
+    down_b((y + 1) % 4)
+    rb.second_right()
+    down_b((y + 3) % 4)
+    rb.second_left()
     down_a((x + 1) % 4)
     ra.second_right()
     down_a((x + 3) % 4)
     ra.second_left()
-    down_b((y + 1) % 4)
-    rb.second_right()
-    down_b((y + 3) % 4)
-    rb.second_left()
     down_c((k + 1) % 4)
     rc.second_right()
     down_c((k + 3) % 4)
     rc.second_left()
+    rc.third()
+    rb.third()
     ra.third()
-    rb.third()
-    rc.third()
     down_a(x)
     down_b(y)
     down_c(k)
@@ -491,43 +491,55 @@
 
     lax.fori_loop(0, 4, own_shared, 0)
 
-    def run(stages):
-        for st in stages:
-            st.first()
-        for st in stages:
-            st.second_right()
-            st.second_left()
-        for st in stages:
-            st.third()
-
-    ra.last()
-    rb.last()
-    rc.last()
     sa = Reduce(links, lambda t, h: PA.at[x, t, two(h)], lambda n: A2.at[n], me.yn, y, add3d, add3_3d)
     sb = Reduce(links, lambda t, h: PB.at[y, t, two(h)], lambda n: B2.at[n], me.zn, k, add3d, add3_3d)
     sc = Reduce(links, lambda t, h: PC.at[k, t, two(h)], lambda n: CC2.at[n], me.xn, x, add3d, add3_3d)
-    run((sa, sb, sc))
-    sa.last()
-    sb.last()
-    sc.last()
     ta = Reduce(links, lambda t, h: PA.at[x, y, t, part_rows(0, h)], last_bufs(0, (A3, A4)), me.zn, k, add2d, add3_2d)
     tb = Reduce(links, lambda t, h: PB.at[y, k, t, part_rows(1, h)], last_bufs(1, (B3, B4)), me.xn, x, add2d, add3_2d)
     tc = Reduce(links, lambda t, h: PC.at[k, x, t, part_rows(2, h)], last_bufs(2, (CC3, CC4)), me.yn, y, add2d, add3_2d)
-    run((ta, tb, tc))
+
+    def enter(before, after):
+        before.last()
+        after.first()
+        after.second_right()
+        after.second_left()
+
+    enter(rc, sc)
+    enter(ra, sa)
+    enter(rb, sb)
+    sc.third()
+    sa.third()
+    sb.third()
+    enter(sc, tc)
+    enter(sa, ta)
+    enter(sb, tb)
+    tc.third()
+    ta.third()
+    tb.third()
+    low = me.zh == 0
+    far = me.zn(4)
+
+    def exchange(own, p, F):
+        rows = pl.ds(OFFS[p], ROWS[p])
+        whole = own[...]
+        lo = whole[:, 0:448].astype(F32)
+        hi = whole[:, 448:896].astype(F32)
+        E[rows] = jnp.where(low, hi, lo).astype(BF16)
+        F[rows] = jnp.where(low, lo, hi)
+        slot = links.slot()
+        links.start(slot, E.at[rows], G.at[rows], far)
+        return slot
+
+    tc.last()
+    slot_c = exchange(PC.at[k, x, y], 2, F)
     ta.last()
+    slot_a = exchange(PA.at[x, y, k], 0, F)
     tb.last()
-    tc.last()
-    F[0:48] = PA[x, y, k]
-    F[48:96] = PB[y, k, x]
-    F[96:128] = PC[k, x, y]
-    lo = F[:, 0:448].astype(F32)
-    hi = F[:, 448:896].astype(F32)
-    low = me.zh == 0
-    E[...] = jnp.where(low, hi, lo).astype(BF16)
-    slot = links.slot()
-    links.start(slot, E, G, me.zn(4))
-    links.wait(slot, G, me.zn(4))
-    out[...] = (jnp.where(low, lo, hi) + G[...].astype(F32)).astype(BF16)
+    slot_b = exchange(PB.at[y, k, x], 1, F)
+    for p, slot in ((2, slot_c), (0, slot_a), (1, slot_b)):
+        rows = pl.ds(OFFS[p], ROWS[p])
+        links.wait(slot, G.at[rows], far)
+        out[rows] = (F[rows] + G[rows].astype(F32)).astype(BF16)
     links.drain()
 
 
@@ -573,7 +585,7 @@
             scratch((3, 32, XC), BF16), scratch((3, 16, XC), BF16),
             scratch((6, 2, 4, 32, XC), BF16), scratch((6, 2, 32, XC), BF16),
             scratch((3, 16, XC), BF16), scratch((3, 16, XC), BF16),
-            scratch((TOK, XC), BF16), scratch((TOK, 448), BF16), scratch((TOK, 448), BF16),
+            scratch((TOK, 448), F32), scratch((TOK, 448), BF16), scratch((TOK, 448), BF16),
             dma((192,)), dma((192,)), dma((8,)), dma((16,)), dma((16,)),
         ],
         compiler_params=pltpu.CompilerParams(collective_id=0, has_side_effects=True, vmem_limit_bytes=63 << 20),

time: 169 us -> 159 us (0.941)
  Pallas kernels: 167 us -> 157 us
    pallas_call x1, Pallas kernels: 167 us -> 157 us  [local(): pl.pallas_call(layer_body, name='expert_layer', out_shape=shape((TOK, 448...]
where the time goes in v4:
time: 159 us
  Pallas kernels  157 us (99%)
  local copies, waits for them, and re-layouts  1.67 us (1%)
    pallas_call x1, Pallas kernels, local(): pl.pallas_call(layer_body, name='expert_layer', out_shape=shape((TOK, 448...  157 us

profile of v4, /device:TPU:8, one launch (start us, length us, event | category | flops | bytes accessed | tf_op | source)
XLA Modules:
  0.0 158.7 jit_solution(481171760264953654)
XLA Ops:
  0.0 157.0 %expert_layer.1 = bf16[128,448]{1,0:T(8,128)(2,1)} custom-call(bf16[128,3584]{1,0:T(8,128)(2,1)} %tokens.1, s32[8,128]{1,0:T(8,128)} %bitcast.8, f32[8,128]{1,0:T(8,128)} %bitcast.9, s32[16]{0:T(128)} %swap.1, bf16[3584,256]{1,0:T(8,128)(2,1)} %bitcast.5, bf16[3584,256]{1,0:T(8,128)(2,1)} %bitcast.6, bf16[256,3584]{1,0:T(8,128)(2,1)} %bitcast.7, ...), custom_call_target="tpu_custom_call" | custom-call | tf_op jit(solution)/shard_map/expert_layer/pallas_call | solution.py:573
  157.1 1.7 %copy.11 = bf16[128,448]{0,1:T(8,128)(2,1)} copy(bf16[128,448]{1,0:T(8,128)(2,1)} %expert_layer.1) | data formatting | bytes 229376 | tf_op jit(solution)/shard_map/expert_layer/pallas_call | solution.py:573

commit v5 on v4

--- a/solution.py
+++ b/solution.py
@@ -14,8 +14,8 @@
 D = 3584
 TOK = 128
 HID = 256
-C1 = (0, 896)
-C2 = (896, 1152)
+C2 = (0, 1152)
+C1 = (1152, 896)
 QBASE, QW = 2048, 384
 ROWS = (48, 48, 32)
 OFFS = (0, 48, 96)
@@ -120,12 +120,11 @@
 
 
 def gather_phase(me, links, tokens, ids, rw, swap, gate, up, down, sgate, sup, sdown, act, DW, S, sem,
-                 X, W, SW, RAW, acc, WT, wt, T):
+                 X, W, SW, RAW, acc, WT, wt):
     x, y, k = me.x, me.y, me.k
     q_me = y * 4 + k
     c1 = pl.ds(C1[0], C1[1])
     c2 = pl.ds(C2[0], C2[1])
-    both = pl.ds(0, QBASE)
     act_a, act_b, act_c = act
     local_sem, wt_send, wt_recv = sem
 
@@ -139,13 +138,11 @@
         copy.start()
         return copy
 
-    own0 = load(tokens.at[:, both], X.at[y, k, :, both], 0)
-    own1 = load(tokens.at[:, qx], X.at[y, k, :, qx], 1)
+    own = load(tokens, X.at[y, k], 0)
     w_gate = load(gate, W.at[0], 2)
     w_up = load(up, W.at[2], 3)
     w_down = load(down, RAW, 4)
     w_sg = load(sgate, SW, 5)
-    w_tok = load(tokens, T, 6)
 
     hops = [me.plane((q_me + d) % 16) for d in range(1, 16)]
     greet(hops + [me.xn(1), me.xn(-1), me.yn(1), me.yn(-1), me.zn(1), me.zn(-1), me.zn(4), me.peer()])
@@ -172,7 +169,8 @@
                   (lambda h: tokens.at[rows(h), c1]) if d == 0 else None) for d in range(4)]
     g2y = [Gather(links, part(lambda s, u, h: X.at[u, s, rows(h), c2], col(d)), me.yn, y,
                   (lambda h: tokens.at[rows(h), c2]) if d == 0 else None) for d in range(4)]
-    g3x = [Gather(links, part(lambda s, u, h: X.at[s, two(h), :, qcol(u)], row(d)), me.xn, x) for d in range(4)]
+    g3x0 = {d: Gather(links, part(lambda s, u, h: X.at[y, s, rows(h), qcol(u)], col(d)), me.xn, x) for d in (1, 3, 2)}
+    g3x = {d: Gather(links, part(lambda s, u, h: X.at[s, two(h), :, qcol(u)], row(d)), me.xn, x) for d in (1, 3, 2)}
 
     def done(g):
         g.near()
@@ -200,6 +198,7 @@
         dots(lambda lo, width: X[u, :, :, lo:lo + width].reshape(4 * TOK, width), write, cols)
 
     QC = (QBASE, D - QBASE)
+    RC = (C1[0], D - C1[0])
 
     g3z[0].send()
     g3y.send()
@@ -218,16 +217,18 @@
             picked = jnp.sum(jnp.where(chosen == stored, mix, 0.0), axis=0, keepdims=True)
             tile = jnp.where(lane_row == r, picked, tile)
         wt[q] = tile
-    own0.wait()
-    own1.wait()
+    own.wait()
     g3z[0].forward()
     g3y.forward()
+    g3z[0].near()
+    g3x0[1].send()
+    g3x0[3].send()
     g1y.send()
     g3y.near()
     g3z[1].send()
     g3z[3].send()
-    done(g3z[0])
-    g3x[0].send()
+    g3z[0].far()
+    g3x0[2].send()
     g3y.far()
     g3z[2].send()
     g2y[0].send()
@@ -242,77 +243,75 @@
     g2z.send()
     g3z[2].forward()
     g1z[0].send()
+    w_sg.wait()
+    sg = jnp.dot(X[y, k], SW[...], preferred_element_type=F32)
+    w_su = load(sup, SW, 5)
+    silu = sg / (1.0 + jnp.exp(-sg))
+    for d in (1, 3, 2):
+        g3x0[d].forward()
+    g1y.forward()
+    done(g3z[1])
+    g3x[1].send()
+    g2z.forward()
+    g1y.near()
+    g1z[1].send()
+    g1y.far()
     w_down.wait()
     for xx in range(4):
         DW[xx, 0:HID] = jnp.concatenate(
             [RAW[:, 448 * xx:448 * xx + 448], RAW[:, 1792 + 448 * xx:1792 + 448 * xx + 448]], axis=1)
     links.start(swap_down, DW.at[:, pl.ds(0, HID)], DW.at[:, pl.ds(HID, HID)], peer)
     w_sdown = load(sdown, RAW, 4)
-    g1y.forward()
-    g3x[0].forward()
-    done(g3z[1])
-    g3x[1].send()
-    g2z.forward()
-    acc[...] = jnp.zeros_like(acc)
-    g1y.near()
-    g1z[1].send()
-    g1y.far()
     done(g3z[3])
     done(g3z[2])
-    w_tok.wait()
-    w_sg.wait()
-    sg = jnp.dot(T[...], SW[...], preferred_element_type=F32)
-    w_su = load(sup, SW, 5)
-    silu = sg / (1.0 + jnp.exp(-sg))
     g2z.near()
     g2y[1].send()
     g2y[0].forward()
     g3x[1].forward()
     g3x[3].send()
+    w_su.wait()
+    sact = (silu * jnp.dot(X[y, k], SW[...], preferred_element_type=F32)).astype(BF16)
+    g2z.far()
     g1z[0].forward()
     g1z[3].send()
-    g2z.far()
-    w_su.wait()
-    sact = (silu * jnp.dot(T[...], SW[...], preferred_element_type=F32)).astype(BF16)
+    acc[...] = jnp.zeros_like(acc)
     w_gate.wait()
     w_up.wait()
     links.wait(swap_gate, W.at[1], peer)
     links.wait(swap_up, W.at[3], peer)
-    done(g3x[0])
-    by_row(y, QC)
+    done(g2y[0])
+    by_column(k, C2)
     g2y[1].forward()
     g2y[3].send()
-    done(g2y[0])
-    by_column(k, C2)
+    g3x[3].forward()
+    g3x[2].send()
+    for d in (1, 3, 2):
+        done(g3x0[d])
+    done(g1z[0])
+    by_row(y, RC)
     g1z[1].forward()
     g1z[2].send()
-    g3x[3].forward()
-    g3x[2].send()
+    done(g2y[1])
+    by_column(col(1), C2)
+    g2y[3].forward()
+    g2y[2].send()
     w_sdown.wait()
     for xx in range(4):
         S[xx] = jnp.concatenate(
             [jnp.dot(sact, RAW[:, base + 448 * xx:base + 448 * xx + 448], preferred_element_type=F32)
              for base in (0, 1792)], axis=1).astype(BF16)
-    done(g1z[0])
-    by_row(y, C1)
-    done(g2y[1])
-    by_column(col(1), C2)
-    g2y[3].forward()
-    g2y[2].send()
+    g1z[3].forward()
     done(g3x[1])
-    by_row(row(1), QC)
-    g1z[3].forward()
     done(g1z[1])
-    by_row(row(1), C1)
+    by_row(row(1), RC)
     g2y[2].forward()
     g3x[2].forward()
     done(g2y[3])
     by_column(col(3), C2)
     g1z[2].forward()
     done(g3x[3])
-    by_row(row(3), QC)
     done(g1z[3])
-    by_row(row(3), C1)
+    by_row(row(3), RC)
     for d in range(1, 16):
         q = (q_me + 16 - d) % 16
         pltpu.make_async_remote_copy(
@@ -554,7 +553,7 @@
         functools.partial(gather_phase, me, links, tokens, ids, rw, swap, gate, up, down, sgate, sup, sdown, act, DW, S,
                           (local_sem, wt_send, wt_recv)),
         vmem((4, 4, TOK, D), BF16), vmem((4, D, HID), BF16), vmem((D, HID), BF16), vmem((HID, D), BF16),
-        vmem((4, 4, 4, TOK, HID), F32), vmem((16, 8, TOK), F32), vmem((16, 8, TOK), F32), vmem((TOK, D), BF16))
+        vmem((4, 4, 4, TOK, HID), F32), vmem((16, 8, TOK), F32), vmem((16, 8, TOK), F32))
     pl.run_scoped(
         functools.partial(reduce_phase, me, links, act, DW, S,
                           ((A1, A2, A3, A4), (B1, B2, B3, B4), (CC1, CC2, CC3, CC4)), F, E, G, out),

time: 159 us -> 158 us (level)
  no operation moved by 1% of the time
where the time goes in v5:
time: 158 us; the launch traced here: 157 us
  Pallas kernels  156 us (99%)
  local copies, waits for them, and re-layouts  1.67 us (1%)
    pallas_call x1, Pallas kernels, local(): pl.pallas_call(layer_body, name='expert_layer', out_shape=shape((TOK, 448...  156 us

profile of v5, /device:TPU:8, one launch (start us, length us, event | category | flops | bytes accessed | tf_op | source)
XLA Modules:
  0.0 157.4 jit_solution(10645091419485205781)
XLA Ops:
  0.0 155.7 %expert_layer.1 = bf16[128,448]{1,0:T(8,128)(2,1)} custom-call(bf16[128,3584]{1,0:T(8,128)(2,1)} %tokens.1, s32[8,128]{1,0:T(8,128)} %bitcast.8, f32[8,128]{1,0:T(8,128)} %bitcast.9, s32[16]{0:T(128)} %swap.1, bf16[3584,256]{1,0:T(8,128)(2,1)} %bitcast.5, bf16[3584,256]{1,0:T(8,128)(2,1)} %bitcast.6, bf16[256,3584]{1,0:T(8,128)(2,1)} %bitcast.7, ...), custom_call_target="tpu_custom_call" | custom-call | tf_op jit(solution)/shard_map/expert_layer/pallas_call | solution.py:572
  155.7 1.7 %copy.11 = bf16[128,448]{0,1:T(8,128)(2,1)} copy(bf16[128,448]{1,0:T(8,128)(2,1)} %expert_layer.1) | data formatting | bytes 229376 | tf_op jit(solution)/shard_map/expert_layer/pallas_call | solution.py:572

commit v6 on v5

--- a/solution.py
+++ b/solution.py
@@ -538,7 +538,8 @@
     for p, slot in ((2, slot_c), (0, slot_a), (1, slot_b)):
         rows = pl.ds(OFFS[p], ROWS[p])
         links.wait(slot, G.at[rows], far)
-        out[rows] = (F[rows] + G[rows].astype(F32)).astype(BF16)
+        F[rows] = F[rows] + G[rows].astype(F32)
+    out[...] = jnp.transpose(F[...]).astype(BF16)
     links.drain()
 
 
@@ -572,7 +573,7 @@
     return pl.pallas_call(
         layer_body,
         name="expert_layer",
-        out_shape=shape((TOK, 448), BF16),
+        out_shape=shape((448, TOK), BF16),
         in_specs=[ANY, VM, VM, pl.BlockSpec(memory_space=pltpu.SMEM), ANY, ANY, ANY, ANY, ANY, ANY],
         out_specs=VM,
         scratch_shapes=[
@@ -588,7 +589,7 @@
             dma((192,)), dma((192,)), dma((8,)), dma((16,)), dma((16,)),
         ],
         compiler_params=pltpu.CompilerParams(collective_id=0, has_side_effects=True, vmem_limit_bytes=63 << 20),
-    )(tokens, expert_ids.T, route_weight.T, pair_swap, expert_gate[0], expert_up[0], expert_down[0], shared_gate, shared_up, shared_down)
+    )(tokens, expert_ids.T, route_weight.T, pair_swap, expert_gate[0], expert_up[0], expert_down[0], shared_gate, shared_up, shared_down).T
 
 
 def solution(mesh):

time: 158 us -> 158 us (level)
    pallas_call x1 -> x0, local copies, waits for them, and re-layouts: 1.67 us -> none  [local(): pl.pallas_call(layer_body, name='expert_layer', out_shape=shape((TOK, 448...]
where the time goes in v6:
time: 158 us; the launch traced here: 157 us
  Pallas kernels  156 us (99%)
    pallas_call x1, Pallas kernels, local(): pl.pallas_call(layer_body, name='expert_layer', out_shape=shape((448, TOK...  156 us

profile of v6, /device:TPU:8, one launch (start us, length us, event | category | flops | bytes accessed | tf_op | source)
XLA Modules:
  0.0 157.4 jit_solution(13413782182711502477)
XLA Ops:
  0.0 155.8 %expert_layer.1 = bf16[448,128]{1,0:T(8,128)(2,1)} custom-call(bf16[128,3584]{1,0:T(8,128)(2,1)} %tokens.1, s32[8,128]{1,0:T(8,128)} %bitcast.10, f32[8,128]{1,0:T(8,128)} %bitcast.11, s32[16]{0:T(128)} %swap.1, bf16[3584,256]{1,0:T(8,128)(2,1)} %bitcast.6, bf16[3584,256]{1,0:T(8,128)(2,1)} %bitcast.7, bf16[256,3584]{1,0:T(8,128)(2,1)} %bitcast.8, ...), custom_call_target="tpu_custom_call" | custom-call | tf_op jit(solution)/shard_map/expert_layer/pallas_call | solution.py:573
  155.8 1.6 copy.12
